TPU v7x, 256 devices: a whole 4x4x8 slice. The times are simulated.
256 devices in a mesh: sector: 32 (over y_lo, z, core), span: 8 (over y_hi, x).
Axes of the slice: x: 4, y: 4 (y_hi: 2, y_lo: 2; y = y_hi * 2 + y_lo), z: 8, core: 2. Of those that a mesh axis runs over, the one named last changes fastest.
Arguments:
- rhs: float32 [11, 7, 64, 64, 128], P(None, None, 'sector', 'span'), may hold values from -6 to 6
- diag_coef: float32 [64, 64, 128], P('sector', 'span'), may hold values from 2 to 4
- face_coef: float32 [3, 64, 64, 128], P(None, 'sector', 'span'), may hold values from 0.2 to 0.6
- time_coef: float32 [64, 64, 128], P('sector', 'span'), may hold values from 0.05 to 0.4
- jac_up: float32 [3, 7, 7], replicated, may hold values from -1.5 to 1.5
- jac_down: float32 [3, 7, 7], replicated, may hold values from -1.5 to 1.5
- wall_mask: int32 [64, 64, 128], P('sector', 'span'), may hold values 0 or 1
- stator_adj: float32 [11, 7, 128, 64], P(None, None, 'sector', 'span'), may hold values from -6 to 6
- owner: int32 [11, 64, 64], P(None, 'sector', 'span'), may hold values from 0 to 126, as said below
- first_panel_share: float32 [11, 64, 64], P(None, 'sector', 'span'), may hold values from 0 to 1
Outputs:
- adjoint_out: float32 [11, 7, 64, 64, 128], P(None, None, 'sector', 'span')
- stator_sens: float32 [11, 7, 128, 64], P(None, None, 'sector', 'span')
Inputs may be any that keep to these rules, and one draw needn't show every extreme that they name: For instance t and an inlet cell in azimuthal block b (cells b * 2 to (b + 1) * 2 - 1), owner and owner + 1 both lie in panel block q = (b + (t * 32) // 10 - t // 10) mod 32, that is between q * 4 and (q + 1) * 4 - 1.
All inputs are finite; a program needn't handle non-finite values. No bound on the sum of `wall_mask` on one device may be relied on, other than what follows from the above.
Results may differ from a plain program's by a relative error of at most 0.0001.
Values sent between devices are 32-bit elements; how exact they have to be, the bound alone decides.
A program may use at most 64 MiB of HBM per device.

v0:
```python
import functools

import jax
import jax.numpy as jnp
import ml_dtypes
import numpy as np
from jax import lax
from jax.experimental import pallas as pl
from jax.experimental.pallas import tpu as pltpu
from jax.sharding import PartitionSpec as P

SWEEPS = 4
NT = 11
NF = 7
ROWS = NT * NF
PAD = 80
NMAT = 7
SPANS = 8
PT = 4
LANES = 128
F32 = jnp.float32
BF16 = jnp.bfloat16
HIGHEST = lax.Precision.HIGHEST
MESH = pl.DeviceIdType.MESH


def constant_tables():
    row = np.arange(PAD)
    col = np.arange(3 * PAD)
    piece, within = col // PAD, col % PAD
    valid_row, valid_col = row < ROWS, within < ROWS
    expand_rows = ((row[:, None] % NF == np.arange(NF)) & valid_row[:, None]).astype(np.float32)
    expand_cols = ((within[None, :] % NF == np.arange(NF)[:, None]) & valid_col).astype(np.float32)
    same_instance = (row[:, None] // NF == within[None, :] // NF) & valid_row[:, None] & valid_col
    instance_rows = ((row[:, None] // NF == np.arange(NT)) & valid_row[:, None]).astype(np.float32)
    step = np.arange(NT)[:, None] - np.arange(NT)[None, :]
    sines = np.where(step == 0, 1.0, np.sin(np.pi * step / NT))
    spectral = np.where(step == 0, 0.0, 0.5 * (1.0 - 2.0 * (step % 2)) / sines)
    time_op = np.zeros((PAD, PAD), np.float32)
    time_op[:ROWS, :ROWS] = np.kron(spectral.T, np.eye(NF))
    high = time_op.astype(ml_dtypes.bfloat16)
    low = (time_op - high.astype(np.float32)).astype(ml_dtypes.bfloat16)
    time_op = np.concatenate([high, high, low], axis=1)
    return expand_rows, expand_cols, same_instance.astype(np.float32), instance_rows, time_op


def shift_of(instance, count):
    return ((instance * count) // (NT - 1) - instance // (NT - 1)) % count


def split(value):
    high = value.astype(BF16)
    low = (value - high.astype(F32)).astype(BF16)
    return high, low


def kernel(
    ns,
    nr,
    rhs,
    diag,
    face,
    time,
    jac_up,
    jac_down,
    wall,
    stator,
    owner,
    share,
    expand_rows,
    expand_cols,
    same_instance,
    instance_rows,
    time_op,
    out,
    sens,
    weights,
    coef,
    base,
    t_buf,
    tu_buf,
    td_buf,
    ru_buf,
    rd_buf,
    xu_buf,
    xd_buf,
    su_buf,
    sd_buf,
    panel_send,
    panel_recv,
    panel_rows,
    panel_weight,
    inlet,
    back_send,
    back_recv,
    theta_send,
    theta_recv,
    span_send,
    span_recv,
    panel_sems,
    back_sems,
):
    sector = lax.axis_index("sector")
    span = lax.axis_index("span")
    shifts = [shift_of(t, ns) for t in range(NT)]
    partners = sorted({d % ns for s in shifts for d in (s, -s)} | {1 % ns, (ns - 1) % ns})
    partners = [d for d in partners if d != 0]

    def at_sector(step):
        return {"sector": lax.rem(sector + step, ns)}

    ru_buf[:, SPANS] = jnp.zeros((SWEEPS,) + ru_buf.shape[2:], F32)
    rd_buf[:, 0] = jnp.zeros((SWEEPS,) + rd_buf.shape[2:], F32)

    barrier = pltpu.get_barrier_semaphore()
    for step in partners:
        pl.semaphore_signal(barrier, inc=1, device_id=at_sector(step), device_id_type=MESH)

    @pl.when(span > 0)
    def _():
        pl.semaphore_signal(barrier, inc=1, device_id={"span": span - 1}, device_id_type=MESH)

    @pl.when(span < nr - 1)
    def _():
        pl.semaphore_signal(barrier, inc=1, device_id={"span": span + 1}, device_id_type=MESH)

    lane = lax.broadcasted_iota(jnp.int32, (PAD, LANES), 1)
    panel_send[...] = jnp.zeros_like(panel_send)
    back_send[...] = jnp.zeros_like(back_send)
    for t in range(NT):
        for p in range(PT):
            panel_send[t, 0:NF, p * SPANS : (p + 1) * SPANS] = stator[t, :, p, :]

    beside = (span > 0).astype(jnp.int32) + (span < nr - 1).astype(jnp.int32)
    pl.semaphore_wait(barrier, len(partners) + beside)

    def panel_copy(t):
        return pltpu.make_async_remote_copy(
            src_ref=panel_send.at[t],
            dst_ref=panel_recv.at[t],
            send_sem=panel_sems.at[0, t],
            recv_sem=panel_sems.at[1, t],
            device_id=at_sector(ns - shifts[t]),
            device_id_type=MESH,
        )

    def back_copy(t):
        return pltpu.make_async_remote_copy(
            src_ref=back_send.at[t],
            dst_ref=back_recv.at[t],
            send_sem=back_sems.at[0, t],
            recv_sem=back_sems.at[1, t],
            device_id=at_sector(shifts[t]),
            device_id_type=MESH,
        )

    for t in range(NT):
        if shifts[t]:
            panel_copy(t).start()

    weights[0:PAD, :] = time_op[...]
    for direction in range(3):
        for side, table in enumerate((jac_up, jac_down)):
            block = jnp.dot(expand_rows[...], table[direction], precision=HIGHEST, preferred_element_type=F32)
            block = jnp.dot(block, expand_cols[...], precision=HIGHEST, preferred_element_type=F32)
            block = block * same_instance[...]
            high, low = split(block)
            piece = lax.broadcasted_iota(jnp.int32, block.shape, 1)
            start = (1 + 2 * direction + side) * PAD
            weights[start : start + PAD, :] = jnp.where(
                piece < 2 * PAD, high.astype(F32), low.astype(F32)
            ).astype(BF16)

    inverse = wall[...].astype(F32) / diag[...]
    axial_lane = lax.broadcasted_iota(jnp.int32, inverse.shape, 1)
    axial = inverse * face[2]
    coef[0] = inverse
    coef[1] = inverse * time[...]
    coef[2] = inverse * face[0]
    coef[3] = inverse * face[1]
    coef[4] = jnp.where(axial_lane == LANES - 1, 0.0, axial)
    coef[5] = jnp.where(axial_lane == 0, 0.0, axial)

    for a in range(2):
        spread = jnp.dot(instance_rows[...], share[:, a, :], precision=HIGHEST, preferred_element_type=F32)
        first = jnp.bitwise_and(owner[:, a, :], PT - 1).astype(F32)
        first = jnp.dot(instance_rows[...], first, preferred_element_type=F32)
        for p in range(PT):
            lower = jnp.where(first == p, spread, 0.0)
            upper = jnp.where(first == p - 1, 1.0 - spread, 0.0)
            panel_weight[a, p, :, 0:SPANS] = lower + upper

    panel_rows[...] = jnp.zeros_like(panel_rows)
    for t in range(NT):
        if shifts[t]:
            panel_copy(t).wait_recv()
            panel_rows[t * NF : (t + 1) * NF, :] = panel_recv[t, 0:NF, :]
        else:
            panel_rows[t * NF : (t + 1) * NF, :] = panel_send[t, 0:NF, :]
    seam = []
    for a in range(2):
        total = jnp.zeros((PAD, LANES), F32)
        for p in range(PT):
            moved = panel_rows[...]
            if p:
                moved = pltpu.roll(moved, LANES - p * SPANS, 1)
            total = total + jnp.where(lane < SPANS, panel_weight[a, p] * moved, 0.0)
        seam.append(total)

    base[...] = jnp.zeros_like(base)
    for r in range(SPANS):
        for a in range(2):
            moved = seam[a] if r == 0 else pltpu.roll(seam[a], LANES - r, 1)
            moved = jnp.where(lane == 0, moved, 0.0)
            plane = rhs[pl.ds(a * SPANS + r, ROWS, stride=2 * SPANS), :] + moved[0:ROWS]
            base[r, a, 0:ROWS, :] = plane * coef[0, a * SPANS + r : a * SPANS + r + 1, :]

    def theta_copies(k, r):
        up = pltpu.make_async_remote_copy(
            src_ref=su_buf.at[k, r],
            dst_ref=tu_buf.at[k, r, 1],
            send_sem=theta_send.at[k, r, 0],
            recv_sem=theta_recv.at[k, r, 0],
            device_id=at_sector(ns - 1),
            device_id_type=MESH,
        )
        down = pltpu.make_async_remote_copy(
            src_ref=sd_buf.at[k, r],
            dst_ref=td_buf.at[k, r, 0],
            send_sem=theta_send.at[k, r, 1],
            recv_sem=theta_recv.at[k, r, 1],
            device_id=at_sector(1),
            device_id_type=MESH,
        )
        return up, down

    def to_lower_span(k):
        return pltpu.make_async_remote_copy(
            src_ref=ru_buf.at[k, 0],
            dst_ref=ru_buf.at[k, SPANS],
            send_sem=span_send.at[k, 0],
            recv_sem=span_recv.at[k, 0],
            device_id={"span": span - 1},
            device_id_type=MESH,
        )

    def to_upper_span(k):
        return pltpu.make_async_remote_copy(
            src_ref=rd_buf.at[k, SPANS],
            dst_ref=rd_buf.at[k, 0],
            send_sem=span_send.at[k, 1],
            recv_sem=span_recv.at[k, 1],
            device_id={"span": span + 1},
            device_id_type=MESH,
        )

    def row_at(i):
        return lax.rem(i, 2) * (SPANS - 1 - 2 * (i // 2)) + i // 2

    def emit(k, r, planes):
        columns = []
        for plane in planes:
            high, low = split(plane)
            columns.append(jnp.concatenate([high, low, high], axis=0))
        data = jnp.concatenate(columns, axis=1)
        product = jnp.dot(weights[...], data, preferred_element_type=F32)

        def part(m, a):
            return product[m * PAD : (m + 1) * PAD, a * LANES : (a + 1) * LANES]

        su_buf[k, r] = part(1, 0)
        sd_buf[k, r] = part(2, 1)
        for copy in theta_copies(k, r):
            copy.start()
        for a in range(2):
            ru_buf[k, r, a] = part(3, a)
            rd_buf[k, r + 1, a] = part(4, a)

        @pl.when((r == 0) & (span > 0))
        def _():
            to_lower_span(k).start()

        @pl.when((r == SPANS - 1) & (span < nr - 1))
        def _():
            to_upper_span(k).start()

        tu_buf[k, r, 0] = part(1, 1)
        td_buf[k, r, 1] = part(2, 0)
        for a in range(2):
            t_buf[k, r, a] = part(0, a)
            xu_buf[k, r, a] = part(5, a)
            xd_buf[k, r, a] = part(6, a)

    def update(k, r):
        for copy in theta_copies(k, r):
            copy.wait_recv()

        @pl.when((r == SPANS - 1) & (span < nr - 1))
        def _():
            to_lower_span(k).wait_recv()

        @pl.when((r == 0) & (span > 0))
        def _():
            to_upper_span(k).wait_recv()

        planes = []
        for a in range(2):

            def coefficient(n):
                return coef[n, pl.ds(a * SPANS + r, 1), :]

            total = base[r, a] - coefficient(1) * t_buf[k, r, a]
            total = total - coefficient(2) * (tu_buf[k, r, a] + td_buf[k, r, a])
            total = total - coefficient(3) * (ru_buf[k, r + 1, a] + rd_buf[k, r, a])
            total = total - coefficient(4) * pltpu.roll(xu_buf[k, r, a], LANES - 1, 1)
            total = total - coefficient(5) * pltpu.roll(xd_buf[k, r, a], 1, 1)
            planes.append(total)
        return planes

    def first(i, carry):
        r = row_at(i)
        emit(0, r, [base[r, a] for a in range(2)])
        return carry

    lax.fori_loop(0, SPANS, first, 0)

    def middle(i, carry):
        k, r = i // SPANS, row_at(lax.rem(i, SPANS))
        emit(k + 1, r, update(k, r))
        return carry

    lax.fori_loop(0, (SWEEPS - 1) * SPANS, middle, 0)

    inlet[...] = jnp.zeros_like(inlet)

    def last(i, carry):
        r = row_at(i)
        planes = update(SWEEPS - 1, r)
        for a in range(2):
            out[pl.ds(a * SPANS + r, ROWS, stride=2 * SPANS), :] = planes[a][0:ROWS]
            inlet[a] = jnp.where(lane == r, pltpu.roll(planes[a], r, 1), inlet[a])
        return carry

    lax.fori_loop(0, SPANS, last, 0)

    back = jnp.zeros((PAD, LANES), F32)
    for p in range(PT):
        total = jnp.zeros((PAD, LANES), F32)
        for a in range(2):
            total = total + panel_weight[a, p] * inlet[a]
        total = jnp.where(lane < SPANS, total, 0.0)
        back = back + (pltpu.roll(total, p * SPANS, 1) if p else total)
    panel_rows[...] = back
    for t in range(NT):
        back_send[t, 0:NF, :] = panel_rows[t * NF : (t + 1) * NF, :]
        if shifts[t]:
            back_copy(t).start()
    for t in range(NT):
        if shifts[t]:
            back_copy(t).wait_recv()
            tile = back_recv[t, 0:NF, :]
        else:
            tile = back_send[t, 0:NF, :]
        for p in range(PT):
            sens[t, :, p, :] = tile[:, p * SPANS : (p + 1) * SPANS]

    for t in range(NT):
        if shifts[t]:
            panel_copy(t).wait_send()
            back_copy(t).wait_send()

    def drain(i, carry):
        k, r = i // SPANS, lax.rem(i, SPANS)
        for copy in theta_copies(k, r):
            copy.wait_send()
        return carry

    lax.fori_loop(0, SWEEPS * SPANS, drain, 0)
    for k in range(SWEEPS):

        @pl.when(span > 0)
        def _():
            to_lower_span(k).wait_send()

        @pl.when(span < nr - 1)
        def _():
            to_upper_span(k).wait_send()


def on_device(ns, nr, rhs, diag_coef, face_coef, time_coef, jac_up, jac_down, wall_mask, stator_adj, owner, share):
    nt, nf, ct, spans, nax = rhs.shape
    tables = constant_tables()
    plane = (SWEEPS, SPANS, 2, PAD, LANES)
    ring = (SWEEPS, SPANS + 1, 2, PAD, LANES)
    edge = (SWEEPS, SPANS, PAD, LANES)
    out, sens = pl.pallas_call(
        functools.partial(kernel, ns, nr),
        out_shape=(
            jax.ShapeDtypeStruct((nt * nf * ct * spans, nax), F32),
            jax.ShapeDtypeStruct(stator_adj.shape, F32),
        ),
        in_specs=[pl.BlockSpec(memory_space=pltpu.VMEM)] * (10 + len(tables)),
        out_specs=(pl.BlockSpec(memory_space=pltpu.VMEM),) * 2,
        scratch_shapes=[
            pltpu.VMEM((NMAT * PAD, 3 * PAD), BF16),
            pltpu.VMEM((6, 2 * SPANS, LANES), F32),
            pltpu.VMEM(plane[1:], F32),
            pltpu.VMEM(plane, F32),
            pltpu.VMEM(plane, F32),
            pltpu.VMEM(plane, F32),
            pltpu.VMEM(ring, F32),
            pltpu.VMEM(ring, F32),
            pltpu.VMEM(plane, F32),
            pltpu.VMEM(plane, F32),
            pltpu.VMEM(edge, F32),
            pltpu.VMEM(edge, F32),
            pltpu.VMEM((NT, 8, LANES), F32),
            pltpu.VMEM((NT, 8, LANES), F32),
            pltpu.VMEM((PAD, LANES), F32),
            pltpu.VMEM((2, PT, PAD, LANES), F32),
            pltpu.VMEM((2, PAD, LANES), F32),
            pltpu.VMEM((NT, 8, LANES), F32),
            pltpu.VMEM((NT, 8, LANES), F32),
            pltpu.SemaphoreType.DMA((SWEEPS, SPANS, 2)),
            pltpu.SemaphoreType.DMA((SWEEPS, SPANS, 2)),
            pltpu.SemaphoreType.DMA((SWEEPS, 2)),
            pltpu.SemaphoreType.DMA((SWEEPS, 2)),
            pltpu.SemaphoreType.DMA((2, NT)),
            pltpu.SemaphoreType.DMA((2, NT)),
        ],
        compiler_params=pltpu.CompilerParams(
            collective_id=0, has_side_effects=True, vmem_limit_bytes=56 * 2**20
        ),
    )(
        rhs.reshape(nt * nf * ct * spans, nax),
        diag_coef.reshape(ct * spans, nax),
        face_coef.reshape(3, ct * spans, nax),
        time_coef.reshape(ct * spans, nax),
        jac_up,
        jac_down,
        wall_mask.reshape(ct * spans, nax),
        stator_adj,
        owner,
        share,
        *tables,
    )
    return out.reshape(rhs.shape), sens


def solution(mesh):
    in_specs = (
        P(None, None, "sector", "span", None),
        P("sector", "span", None),
        P(None, "sector", "span", None),
        P("sector", "span", None),
        P(),
        P(),
        P("sector", "span", None),
        P(None, None, "sector", "span"),
        P(None, "sector", "span"),
        P(None, "sector", "span"),
    )
    out_specs = (P(None, None, "sector", "span", None), P(None, None, "sector", "span"))
    return jax.shard_map(
        functools.partial(on_device, mesh.shape["sector"], mesh.shape["span"]),
        mesh=mesh,
        in_specs=in_specs,
        out_specs=out_specs,
        check_vma=False,
    )
```

profile of v0, /device:TPU:7, one launch (start us, length us, event | category | flops | bytes accessed | tf_op | source)
XLA Modules:
  0.0 57.9 jit_solution(17794041877017650347)
XLA Ops:
  0.6 0.0 copy-start
  0.6 0.7 %copy-done = s32[11,2,8]{0,2,1:T(8,128)S(1)} copy-done((s32[11,2,8]{0,2,1:T(8,128)S(1)}, s32[11,2,8]{0,2,1:T(8,128)}, u32[]{:S(2)}) %copy-start) | copy-done | bytes 728
  1.3 0.0 copy-start.1
  1.3 0.7 %copy.18.owner = s32[11,2,8]{2,1,0:T(2,128)} copy(s32[11,2,8]{0,2,1:T(8,128)S(1)} %copy-done) | data formatting | bytes 1408 | tf_op args[8]
  2.0 0.0 copy-done.1
  2.0 0.7 %copy.19.share = f32[11,2,8]{2,1,0:T(2,128)} copy(f32[11,2,8]{0,2,1:T(8,128)S(1)} %copy-done.1) | data formatting | bytes 1408 | tf_op args[9]
  2.7 1.8 %copy.17.stator = f32[11,7,4,8]{3,2,1,0:T(4,128)} copy(f32[11,7,4,8]{0,3,2,1:T(8,128)} %param.22) | data formatting | bytes 19712 | tf_op args[7]
  4.5 49.6 %shard_map.158 = (f32[1232,128]{1,0:T(8,128)}, f32[11,7,4,8]{3,2,1,0:T(4,128)}) custom-call(f32[1232,128]{1,0:T(8,128)} %bitcast.7, f32[16,128]{1,0:T(8,128)} %bitcast.9, f32[3,16,128]{2,1,0:T(8,128)} %bitcast.8, f32[16,128]{1,0:T(8,128)} %bitcast.10, f32[3,7,7]{2,1,0:T(8,128)} %jac_up.1, f32[3,7,7]{2,1,0:T(8,128)} %jac_down.1, s32[16,128]{1,0:T(8,128)} %bitcast.11, ...), custom_call_target="tpu_custom_call" | custom-call | tf_op jit(solution)/shard_map/pallas_call | solution.py:396
  54.1 1.8 %copy.20 = f32[11,7,4,8]{0,3,2,1:T(8,128)} copy(f32[11,7,4,8]{3,2,1,0:T(4,128)} %get-tuple-element.7) | data formatting | bytes 19712
  55.9 1.9 %copy.22 = f32[11,7,2,8,128]{4,3,2,1,0:T(8,128)} copy(f32[11,7,2,8,128]{4,3,2,1,0:T(8,128)} %bitcast.6) | data formatting | bytes 1261568
Async XLA Ops:
  0.6 0.7 %copy-start = (s32[11,2,8]{0,2,1:T(8,128)S(1)}, s32[11,2,8]{0,2,1:T(8,128)}, u32[]{:S(2)}) copy-start(s32[11,2,8]{0,2,1:T(8,128)} %param.23) | copy-start | bytes 2116
  1.3 0.7 %copy-start.1 = (f32[11,2,8]{0,2,1:T(8,128)S(1)}, f32[11,2,8]{0,2,1:T(8,128)}, u32[]{:S(2)}) copy-start(f32[11,2,8]{0,2,1:T(8,128)} %param.24) | copy-start | bytes 2116
where the time goes:
time: 58.2 us; the launch traced here: 57.9 us
  Pallas kernels  49.6 us (85%)
  local copies, waits for them, and re-layouts  7.59 us (13%)
  between operations  0.65 us (1%)
    pallas_call x1, Pallas kernels, on_device(): pl.pallas_call(functools.partial(kernel, ns, nr), out_shape=(jax.ShapeDty...  49.6 us
    unnamed x9, local copies, waits for them, and re-layouts  7.59 us

commit v1 on v0

--- a/solution.py
+++ b/solution.py
@@ -18,30 +18,22 @@
 SPANS = 8
 PT = 4
 LANES = 128
+WIDE = 256
 F32 = jnp.float32
 BF16 = jnp.bfloat16
 HIGHEST = lax.Precision.HIGHEST
 MESH = pl.DeviceIdType.MESH
 
 
-def constant_tables():
-    row = np.arange(PAD)
-    col = np.arange(3 * PAD)
-    piece, within = col // PAD, col % PAD
-    valid_row, valid_col = row < ROWS, within < ROWS
-    expand_rows = ((row[:, None] % NF == np.arange(NF)) & valid_row[:, None]).astype(np.float32)
-    expand_cols = ((within[None, :] % NF == np.arange(NF)[:, None]) & valid_col).astype(np.float32)
-    same_instance = (row[:, None] // NF == within[None, :] // NF) & valid_row[:, None] & valid_col
-    instance_rows = ((row[:, None] // NF == np.arange(NT)) & valid_row[:, None]).astype(np.float32)
+def time_operator():
     step = np.arange(NT)[:, None] - np.arange(NT)[None, :]
     sines = np.where(step == 0, 1.0, np.sin(np.pi * step / NT))
     spectral = np.where(step == 0, 0.0, 0.5 * (1.0 - 2.0 * (step % 2)) / sines)
-    time_op = np.zeros((PAD, PAD), np.float32)
-    time_op[:ROWS, :ROWS] = np.kron(spectral.T, np.eye(NF))
-    high = time_op.astype(ml_dtypes.bfloat16)
-    low = (time_op - high.astype(np.float32)).astype(ml_dtypes.bfloat16)
-    time_op = np.concatenate([high, high, low], axis=1)
-    return expand_rows, expand_cols, same_instance.astype(np.float32), instance_rows, time_op
+    table = np.zeros((PAD, PAD), np.float32)
+    table[:ROWS, :ROWS] = np.kron(spectral.T, np.eye(NF))
+    high = table.astype(ml_dtypes.bfloat16)
+    low = (table - high.astype(np.float32)).astype(ml_dtypes.bfloat16)
+    return np.concatenate([high, high, low], axis=1)
 
 
 def shift_of(instance, count):
@@ -54,52 +46,52 @@
     return high, low
 
 
-def kernel(
-    ns,
-    nr,
-    rhs,
-    diag,
-    face,
-    time,
-    jac_up,
-    jac_down,
-    wall,
-    stator,
-    owner,
-    share,
-    expand_rows,
-    expand_cols,
-    same_instance,
-    instance_rows,
-    time_op,
-    out,
-    sens,
-    weights,
-    coef,
-    base,
-    t_buf,
-    tu_buf,
-    td_buf,
-    ru_buf,
-    rd_buf,
-    xu_buf,
-    xd_buf,
-    su_buf,
-    sd_buf,
-    panel_send,
-    panel_recv,
-    panel_rows,
-    panel_weight,
-    inlet,
-    back_send,
-    back_recv,
-    theta_send,
-    theta_recv,
-    span_send,
-    span_recv,
-    panel_sems,
-    back_sems,
-):
+def index_of(shape, dim):
+    return lax.broadcasted_iota(jnp.int32, shape, dim).astype(F32)
+
+
+def over_fields(rows):
+    instance = jnp.floor((rows + 0.5) * (1.0 / NF))
+    return instance, rows - NF * instance
+
+
+def exact_dot(left, right):
+    return jnp.dot(left, right, precision=HIGHEST, preferred_element_type=F32)
+
+
+def kernel(ns, nr, *refs):
+    hbm, refs = refs[:11], refs[11:]
+    (out, sens), refs = refs[:2], refs[2:]
+    vmem, refs = refs[:11], refs[11:]
+    rhs, diag, face, time, jac_up, jac_down, wall, stator, owner, share, time_op = vmem
+    (
+        weights,
+        coef,
+        base,
+        t_buf,
+        tu_buf,
+        td_buf,
+        ru_buf,
+        rd_buf,
+        xu_buf,
+        xd_buf,
+        su_buf,
+        sd_buf,
+        panel_send,
+        panel_recv,
+        panel_rows,
+        panel_weight,
+        inlet,
+        back_send,
+        back_recv,
+        input_sems,
+        theta_send,
+        theta_recv,
+        span_send,
+        span_recv,
+        panel_sems,
+        back_sems,
+    ) = refs
     sector = lax.axis_index("sector")
     span = lax.axis_index("span")
     shifts = [shift_of(t, ns) for t in range(NT)]
@@ -109,6 +101,12 @@
     def at_sector(step):
         return {"sector": lax.rem(sector + step, ns)}
 
+    def load(n):
+        return pltpu.make_async_copy(hbm[n], vmem[n], input_sems.at[n])
+
+    for n in (7, 0, 1, 6, 8, 9, 4, 5, 10, 2, 3):
+        load(n).start()
+
     ru_buf[:, SPANS] = jnp.zeros((SWEEPS,) + ru_buf.shape[2:], F32)
     rd_buf[:, 0] = jnp.zeros((SWEEPS,) + rd_buf.shape[2:], F32)
 
@@ -124,12 +122,12 @@
     def _():
         pl.semaphore_signal(barrier, inc=1, device_id={"span": span + 1}, device_id_type=MESH)
 
-    lane = lax.broadcasted_iota(jnp.int32, (PAD, LANES), 1)
-    panel_send[...] = jnp.zeros_like(panel_send)
-    back_send[...] = jnp.zeros_like(back_send)
+    wide = (NT, WIDE)
+    load(7).wait()
+    panel_rows[...] = jnp.zeros_like(panel_rows)
+    panel_rows[0:NT, 0 : NF * PT * SPANS] = jnp.transpose(stator[...])
     for t in range(NT):
-        for p in range(PT):
-            panel_send[t, 0:NF, p * SPANS : (p + 1) * SPANS] = stator[t, :, p, :]
+        panel_send[t, 0:1, :] = panel_rows[t : t + 1, :]
 
     beside = (span > 0).astype(jnp.int32) + (span < nr - 1).astype(jnp.int32)
     pl.semaphore_wait(barrier, len(partners) + beside)
@@ -158,12 +156,37 @@
         if shifts[t]:
             panel_copy(t).start()
 
+    lane = lax.broadcasted_iota(jnp.int32, (PAD, LANES), 1)
+    row = index_of((PAD, 3 * PAD), 0)
+    column = index_of((PAD, 3 * PAD), 1)
+    column = column - PAD * jnp.floor((column + 0.5) * (1.0 / PAD))
+    row_instance, _ = over_fields(row)
+    column_instance, _ = over_fields(column)
+    same_instance = (row_instance == column_instance) & (row < ROWS) & (column < ROWS)
+    _, row_field = over_fields(index_of((PAD, NF), 0))
+    expand_rows = jnp.where(row_field == index_of((PAD, NF), 1), 1.0, 0.0)
+    column = index_of((NF, 3 * PAD), 1)
+    column = column - PAD * jnp.floor((column + 0.5) * (1.0 / PAD))
+    expand_columns = jnp.where(over_fields(column)[1] == index_of((NF, 3 * PAD), 0), 1.0, 0.0)
+    instance_rows = jnp.where(
+        (over_fields(index_of((PAD, NT), 0))[0] == index_of((PAD, NT), 1)) & (index_of((PAD, NT), 0) < ROWS), 1.0, 0.0
+    )
+    instance_columns = jnp.where(
+        (over_fields(index_of((NT, PAD), 1))[0] == index_of((NT, PAD), 0)) & (index_of((NT, PAD), 1) < ROWS), 1.0, 0.0
+    )
+    wide_lane = lax.broadcasted_iota(jnp.int32, (PAD, WIDE), 1)
+    wide_field = lax.shift_right_logical(wide_lane, 5).astype(F32)
+    same_field = over_fields(index_of((PAD, WIDE), 0))[1] == wide_field
+    lane_panel = jnp.bitwise_and(lax.shift_right_logical(lax.broadcasted_iota(jnp.int32, wide, 1), 3), PT - 1)
+
+    load(4).wait()
+    load(5).wait()
+    load(10).wait()
     weights[0:PAD, :] = time_op[...]
     for direction in range(3):
         for side, table in enumerate((jac_up, jac_down)):
-            block = jnp.dot(expand_rows[...], table[direction], precision=HIGHEST, preferred_element_type=F32)
-            block = jnp.dot(block, expand_cols[...], precision=HIGHEST, preferred_element_type=F32)
-            block = block * same_instance[...]
+            block = exact_dot(exact_dot(expand_rows, table[direction]), expand_columns)
+            block = jnp.where(same_instance, block, 0.0)
             high, low = split(block)
             piece = lax.broadcasted_iota(jnp.int32, block.shape, 1)
             start = (1 + 2 * direction + side) * PAD
@@ -171,6 +194,8 @@
                 piece < 2 * PAD, high.astype(F32), low.astype(F32)
             ).astype(BF16)
 
+    for n in (0, 1, 2, 3, 6, 8, 9):
+        load(n).wait()
     inverse = wall[...].astype(F32) / diag[...]
     axial_lane = lax.broadcasted_iota(jnp.int32, inverse.shape, 1)
     axial = inverse * face[2]
@@ -181,39 +206,49 @@
     coef[4] = jnp.where(axial_lane == LANES - 1, 0.0, axial)
     coef[5] = jnp.where(axial_lane == 0, 0.0, axial)
 
+    spread_lanes = lax.broadcasted_iota(jnp.int32, (SPANS, WIDE), 1)
+    spread_span = jnp.where(
+        jnp.bitwise_and(spread_lanes, SPANS - 1) == lax.broadcasted_iota(jnp.int32, (SPANS, WIDE), 0), 1.0, 0.0
+    )
     for a in range(2):
-        spread = jnp.dot(instance_rows[...], share[:, a, :], precision=HIGHEST, preferred_element_type=F32)
-        first = jnp.bitwise_and(owner[:, a, :], PT - 1).astype(F32)
-        first = jnp.dot(instance_rows[...], first, preferred_element_type=F32)
-        for p in range(PT):
-            lower = jnp.where(first == p, spread, 0.0)
-            upper = jnp.where(first == p - 1, 1.0 - spread, 0.0)
-            panel_weight[a, p, :, 0:SPANS] = lower + upper
-
-    panel_rows[...] = jnp.zeros_like(panel_rows)
+        cells = pl.ds(a * SPANS, SPANS)
+        share_wide = exact_dot(jnp.transpose(share[cells, :]), spread_span)
+        first = jnp.bitwise_and(owner[cells, :], PT - 1).astype(F32)
+        first_wide = exact_dot(jnp.transpose(first), spread_span)
+        own_panel = lane_panel.astype(F32)
+        lower = jnp.where(first_wide == own_panel, share_wide, 0.0)
+        upper = jnp.where(first_wide == own_panel - 1.0, 1.0 - share_wide, 0.0)
+        panel_weight[a] = lower + upper
+
     for t in range(NT):
         if shifts[t]:
             panel_copy(t).wait_recv()
-            panel_rows[t * NF : (t + 1) * NF, :] = panel_recv[t, 0:NF, :]
-        else:
-            panel_rows[t * NF : (t + 1) * NF, :] = panel_send[t, 0:NF, :]
-    seam = []
+            panel_rows[t : t + 1, :] = panel_recv[t, 0:1, :]
+    cells_wide = jnp.zeros(wide, F32)
     for a in range(2):
-        total = jnp.zeros((PAD, LANES), F32)
-        for p in range(PT):
-            moved = panel_rows[...]
-            if p:
-                moved = pltpu.roll(moved, LANES - p * SPANS, 1)
-            total = total + jnp.where(lane < SPANS, panel_weight[a, p] * moved, 0.0)
-        seam.append(total)
+        shares = panel_weight[a] * panel_rows[0:NT, :]
+        shares = shares + pltpu.roll(shares, WIDE - SPANS, 1)
+        shares = shares + pltpu.roll(shares, WIDE - 2 * SPANS, 1)
+        if a:
+            shares = pltpu.roll(shares, a * SPANS, 1)
+        cells_wide = jnp.where(lane_panel == a, shares, cells_wide)
+    spread = jnp.where(same_field, exact_dot(instance_rows, cells_wide), 0.0)
+    gather_cells = jnp.where(
+        jnp.bitwise_and(lax.broadcasted_iota(jnp.int32, (WIDE, LANES), 0), 4 * SPANS - 1)
+        == lax.broadcasted_iota(jnp.int32, (WIDE, LANES), 1),
+        1.0,
+        0.0,
+    )
+    seam = exact_dot(spread, gather_cells)
 
     base[...] = jnp.zeros_like(base)
     for r in range(SPANS):
         for a in range(2):
-            moved = seam[a] if r == 0 else pltpu.roll(seam[a], LANES - r, 1)
+            cell = a * SPANS + r
+            moved = pltpu.roll(seam, LANES - cell, 1) if cell else seam
             moved = jnp.where(lane == 0, moved, 0.0)
-            plane = rhs[pl.ds(a * SPANS + r, ROWS, stride=2 * SPANS), :] + moved[0:ROWS]
-            base[r, a, 0:ROWS, :] = plane * coef[0, a * SPANS + r : a * SPANS + r + 1, :]
+            plane = rhs[pl.ds(cell, ROWS, stride=2 * SPANS), :] + moved[0:ROWS]
+            base[r, a, 0:ROWS, :] = plane * coef[0, cell : cell + 1, :]
 
     def theta_copies(k, r):
         up = pltpu.make_async_remote_copy(
@@ -337,32 +372,27 @@
         r = row_at(i)
         planes = update(SWEEPS - 1, r)
         for a in range(2):
-            out[pl.ds(a * SPANS + r, ROWS, stride=2 * SPANS), :] = planes[a][0:ROWS]
-            inlet[a] = jnp.where(lane == r, pltpu.roll(planes[a], r, 1), inlet[a])
+            out[a * SPANS + r] = planes[a]
+            inlet[...] = jnp.where(lane == a * SPANS + r, pltpu.roll(planes[a], a * SPANS + r, 1), inlet[...])
         return carry
 
     lax.fori_loop(0, SPANS, last, 0)
 
-    back = jnp.zeros((PAD, LANES), F32)
-    for p in range(PT):
-        total = jnp.zeros((PAD, LANES), F32)
-        for a in range(2):
-            total = total + panel_weight[a, p] * inlet[a]
-        total = jnp.where(lane < SPANS, total, 0.0)
-        back = back + (pltpu.roll(total, p * SPANS, 1) if p else total)
-    panel_rows[...] = back
+    back = jnp.zeros(wide, F32)
+    for a in range(2):
+        spread = exact_dot(inlet[:, a * SPANS : (a + 1) * SPANS], spread_span)
+        spread = jnp.where(same_field, spread, 0.0)
+        back = back + panel_weight[a] * exact_dot(instance_columns, spread)
+    panel_rows[0:NT, :] = back
     for t in range(NT):
-        back_send[t, 0:NF, :] = panel_rows[t * NF : (t + 1) * NF, :]
         if shifts[t]:
+            back_send[t, 0:1, :] = panel_rows[t : t + 1, :]
             back_copy(t).start()
     for t in range(NT):
         if shifts[t]:
             back_copy(t).wait_recv()
-            tile = back_recv[t, 0:NF, :]
-        else:
-            tile = back_send[t, 0:NF, :]
-        for p in range(PT):
-            sens[t, :, p, :] = tile[:, p * SPANS : (p + 1) * SPANS]
+            panel_rows[t : t + 1, :] = back_recv[t, 0:1, :]
+    sens[...] = jnp.transpose(panel_rows[0:NT, 0 : NF * PT * SPANS])
 
     for t in range(NT):
         if shifts[t]:
@@ -387,21 +417,44 @@
             to_upper_span(k).wait_send()
 
 
+def store(planes, table, out, sens, sems):
+    copies = [pltpu.make_async_copy(table, sens, sems.at[2 * SPANS])]
+    for cell in range(2 * SPANS):
+        copies.append(pltpu.make_async_copy(planes.at[cell, 0:ROWS], out.at[:, cell], sems.at[cell]))
+    for copy in copies:
+        copy.start()
+    for copy in copies:
+        copy.wait()
+
+
 def on_device(ns, nr, rhs, diag_coef, face_coef, time_coef, jac_up, jac_down, wall_mask, stator_adj, owner, share):
     nt, nf, ct, spans, nax = rhs.shape
-    tables = constant_tables()
     plane = (SWEEPS, SPANS, 2, PAD, LANES)
     ring = (SWEEPS, SPANS + 1, 2, PAD, LANES)
     edge = (SWEEPS, SPANS, PAD, LANES)
-    out, sens = pl.pallas_call(
+    inputs = (
+        rhs.reshape(nt * nf * ct * spans, nax),
+        diag_coef.reshape(ct * spans, nax),
+        face_coef.reshape(3, ct * spans, nax),
+        time_coef.reshape(ct * spans, nax),
+        jac_up,
+        jac_down,
+        wall_mask.reshape(ct * spans, nax),
+        stator_adj.transpose(1, 2, 3, 0).reshape(nf * PT * spans, nt),
+        owner.transpose(1, 2, 0).reshape(ct * spans, nt),
+        share.transpose(1, 2, 0).reshape(ct * spans, nt),
+        jnp.asarray(time_operator()),
+    )
+    planes, table = pl.pallas_call(
         functools.partial(kernel, ns, nr),
         out_shape=(
-            jax.ShapeDtypeStruct((nt * nf * ct * spans, nax), F32),
-            jax.ShapeDtypeStruct(stator_adj.shape, F32),
+            pltpu.VMEM((ct * spans, PAD, nax), F32),
+            pltpu.VMEM((nf * PT * spans, nt), F32),
         ),
-        in_specs=[pl.BlockSpec(memory_space=pltpu.VMEM)] * (10 + len(tables)),
+        in_specs=[pl.BlockSpec(memory_space=pltpu.HBM)] * len(inputs),
         out_specs=(pl.BlockSpec(memory_space=pltpu.VMEM),) * 2,
-        scratch_shapes=[
+        scratch_shapes=[pltpu.VMEM(x.shape, x.dtype) for x in inputs]
+        + [
             pltpu.VMEM((NMAT * PAD, 3 * PAD), BF16),
             pltpu.VMEM((6, 2 * SPANS, LANES), F32),
             pltpu.VMEM(plane[1:], F32),
@@ -414,13 +467,14 @@
             pltpu.VMEM(plane, F32),
             pltpu.VMEM(edge, F32),
             pltpu.VMEM(edge, F32),
-            pltpu.VMEM((NT, 8, LANES), F32),
-            pltpu.VMEM((NT, 8, LANES), F32),
+            pltpu.VMEM((NT, 1, WIDE), F32),
+            pltpu.VMEM((NT, 1, WIDE), F32),
+            pltpu.VMEM((16, WIDE), F32),
+            pltpu.VMEM((2, NT, WIDE), F32),
             pltpu.VMEM((PAD, LANES), F32),
-            pltpu.VMEM((2, PT, PAD, LANES), F32),
-            pltpu.VMEM((2, PAD, LANES), F32),
-            pltpu.VMEM((NT, 8, LANES), F32),
-            pltpu.VMEM((NT, 8, LANES), F32),
+            pltpu.VMEM((NT, 1, WIDE), F32),
+            pltpu.VMEM((NT, 1, WIDE), F32),
+            pltpu.SemaphoreType.DMA((len(inputs),)),
             pltpu.SemaphoreType.DMA((SWEEPS, SPANS, 2)),
             pltpu.SemaphoreType.DMA((SWEEPS, SPANS, 2)),
             pltpu.SemaphoreType.DMA((SWEEPS, 2)),
@@ -429,21 +483,20 @@
             pltpu.SemaphoreType.DMA((2, NT)),
         ],
         compiler_params=pltpu.CompilerParams(
-            collective_id=0, has_side_effects=True, vmem_limit_bytes=56 * 2**20
+            collective_id=0, has_side_effects=True, vmem_limit_bytes=60 * 2**20
         ),
-    )(
-        rhs.reshape(nt * nf * ct * spans, nax),
-        diag_coef.reshape(ct * spans, nax),
-        face_coef.reshape(3, ct * spans, nax),
-        time_coef.reshape(ct * spans, nax),
-        jac_up,
-        jac_down,
-        wall_mask.reshape(ct * spans, nax),
-        stator_adj,
-        owner,
-        share,
-        *tables,
-    )
+    )(*inputs)
+    out, sens = pl.pallas_call(
+        store,
+        out_shape=(
+            jax.ShapeDtypeStruct((nt * nf, ct * spans, nax), F32),
+            jax.ShapeDtypeStruct((nf * PT * spans, nt), F32),
+        ),
+        in_specs=[pl.BlockSpec(memory_space=pltpu.VMEM)] * 2,
+        out_specs=(pl.BlockSpec(memory_space=pltpu.HBM),) * 2,
+        scratch_shapes=[pltpu.SemaphoreType.DMA((2 * SPANS + 1,))],
+    )(pltpu.with_memory_space_constraint(planes, pltpu.VMEM), pltpu.with_memory_space_constraint(table, pltpu.VMEM))
+    sens = sens.reshape(nf, PT, spans, nt).transpose(3, 0, 1, 2)
     return out.reshape(rhs.shape), sens
 
 

time: 58.2 us -> 49.6 us (0.85)
  local copies, waits for them, and re-layouts: 7.59 us -> 0 us
  Pallas kernels: 49.6 us -> 48.8 us
    unnamed x9 -> x0, local copies, waits for them, and re-layouts: 7.59 us -> none
    pallas_call x1 -> x2, Pallas kernels: 49.6 us -> 48.8 us  [the longest x1 47.8 us: on_device(): pl.pallas_call(functools.partial(kernel, ns, nr), out_shape=(pltpu.VMEM((...]
where the time goes in v1:
time: 49.6 us; the launch traced here: 49.5 us
  Pallas kernels  48.8 us (98%)
  between operations  0.64 us (1%)
    pallas_call x1, Pallas kernels, on_device(): pl.pallas_call(functools.partial(kernel, ns, nr), out_shape=(pltpu.VMEM((...  47.8 us
    pallas_call x1, Pallas kernels, on_device(): pl.pallas_call(store, out_shape=(jax.ShapeDtypeStruct((nt * nf, ct * span...  1 us

profile of v1, /device:TPU:7, one launch (start us, length us, event | category | flops | bytes accessed | tf_op | source)
XLA Modules:
  0.0 49.5 jit_solution(7126684113840480231)
XLA Ops:
  0.6 47.8 %shard_map.122 = (f32[16,80,128]{2,1,0:T(8,128)S(1)}, f32[224,11]{1,0:T(8,128)S(1)}) custom-call(f32[1232,128]{1,0:T(8,128)} %bitcast.18, f32[16,128]{1,0:T(8,128)} %bitcast.21, f32[3,16,128]{2,1,0:T(8,128)} %bitcast.20, f32[16,128]{1,0:T(8,128)} %bitcast.22, f32[3,7,7]{2,1,0:T(8,128)} %refs_4_.1, f32[3,7,7]{2,1,0:T(8,128)} %refs_5_.1, s32[16,128]{1,0:T(8,128)} %bitcast.23, ...), custom_call_target="tpu_custom_call" | custom-call | tf_op jit(solution)/shard_map/pallas_call | solution.py:448
  48.5 1.0 %shard_map.123 = (f32[77,16,128]{2,1,0:T(8,128)}, f32[224,11]{1,0:T(8,128)}) custom-call(f32[16,80,128]{2,1,0:T(8,128)S(1)} %get-tuple-element.6.planes, f32[224,11]{1,0:T(8,128)S(1)} %get-tuple-element.7.table), custom_call_target="tpu_custom_call" | custom-call | tf_op jit(solution)/shard_map/pallas_call | solution.py:489

commit v2 on v1

--- a/solution.py
+++ b/solution.py
@@ -84,6 +84,11 @@
         inlet,
         back_send,
         back_recv,
+        jac_rows,
+        delta_send,
+        delta_recv,
+        delta_columns,
+        delta_shift,
         input_sems,
         theta_send,
         theta_recv,
@@ -91,6 +96,7 @@
         span_recv,
         panel_sems,
         back_sems,
+        delta_sems,
     ) = refs
     sector = lax.axis_index("sector")
     span = lax.axis_index("span")
@@ -110,6 +116,8 @@
     ru_buf[:, SPANS] = jnp.zeros((SWEEPS,) + ru_buf.shape[2:], F32)
     rd_buf[:, 0] = jnp.zeros((SWEEPS,) + rd_buf.shape[2:], F32)
 
+    delta_recv[...] = jnp.zeros_like(delta_recv)
+
     barrier = pltpu.get_barrier_semaphore()
     for step in partners:
         pl.semaphore_signal(barrier, inc=1, device_id=at_sector(step), device_id_type=MESH)
@@ -128,9 +136,6 @@
     panel_rows[0:NT, 0 : NF * PT * SPANS] = jnp.transpose(stator[...])
     for t in range(NT):
         panel_send[t, 0:1, :] = panel_rows[t : t + 1, :]
-
-    beside = (span > 0).astype(jnp.int32) + (span < nr - 1).astype(jnp.int32)
-    pl.semaphore_wait(barrier, len(partners) + beside)
 
     def panel_copy(t):
         return pltpu.make_async_remote_copy(
@@ -152,10 +157,6 @@
             device_id_type=MESH,
         )
 
-    for t in range(NT):
-        if shifts[t]:
-            panel_copy(t).start()
-
     lane = lax.broadcasted_iota(jnp.int32, (PAD, LANES), 1)
     row = index_of((PAD, 3 * PAD), 0)
     column = index_of((PAD, 3 * PAD), 1)
@@ -163,11 +164,6 @@
     row_instance, _ = over_fields(row)
     column_instance, _ = over_fields(column)
     same_instance = (row_instance == column_instance) & (row < ROWS) & (column < ROWS)
-    _, row_field = over_fields(index_of((PAD, NF), 0))
-    expand_rows = jnp.where(row_field == index_of((PAD, NF), 1), 1.0, 0.0)
-    column = index_of((NF, 3 * PAD), 1)
-    column = column - PAD * jnp.floor((column + 0.5) * (1.0 / PAD))
-    expand_columns = jnp.where(over_fields(column)[1] == index_of((NF, 3 * PAD), 0), 1.0, 0.0)
     instance_rows = jnp.where(
         (over_fields(index_of((PAD, NT), 0))[0] == index_of((PAD, NT), 1)) & (index_of((PAD, NT), 0) < ROWS), 1.0, 0.0
     )
@@ -182,17 +178,25 @@
     load(4).wait()
     load(5).wait()
     load(10).wait()
-    weights[0:PAD, :] = time_op[...]
+    jac_rows[...] = jnp.zeros_like(jac_rows)
     for direction in range(3):
         for side, table in enumerate((jac_up, jac_down)):
-            block = exact_dot(exact_dot(expand_rows, table[direction]), expand_columns)
-            block = jnp.where(same_instance, block, 0.0)
-            high, low = split(block)
-            piece = lax.broadcasted_iota(jnp.int32, block.shape, 1)
-            start = (1 + 2 * direction + side) * PAD
-            weights[start : start + PAD, :] = jnp.where(
-                piece < 2 * PAD, high.astype(F32), low.astype(F32)
-            ).astype(BF16)
+            start = (2 * direction + side) * 8
+            jac_rows[start : start + NF, 0:NF] = table[direction]
+    high, low = split(jac_rows[...])
+    wide_columns = index_of((8, 3 * PAD), 1)
+    piece = jnp.floor((wide_columns + 0.5) * (1.0 / PAD))
+    chosen = over_fields(wide_columns - PAD * piece)[1] == index_of((8, 3 * PAD), 0)
+    pick_high = jnp.where(chosen & (piece < 2.0), 1.0, 0.0).astype(BF16)
+    pick_low = jnp.where(chosen & (piece > 1.0), 1.0, 0.0).astype(BF16)
+    columns = jnp.dot(high, pick_high, preferred_element_type=F32)
+    columns = (columns + jnp.dot(low, pick_low, preferred_element_type=F32)).astype(BF16)
+    _, field_of_row = over_fields(index_of((PAD, 8), 0))
+    pick_row = jnp.where(field_of_row == index_of((PAD, 8), 1), 1.0, 0.0).astype(BF16)
+    weights[0:PAD, :] = time_op[...]
+    for m in range(1, NMAT):
+        block = jnp.dot(pick_row, columns[8 * (m - 1) : 8 * m, :], preferred_element_type=F32)
+        weights[m * PAD : (m + 1) * PAD, :] = jnp.where(same_instance, block, 0.0).astype(BF16)
 
     for n in (0, 1, 2, 3, 6, 8, 9):
         load(n).wait()
@@ -205,6 +209,14 @@
     coef[3] = inverse * face[1]
     coef[4] = jnp.where(axial_lane == LANES - 1, 0.0, axial)
     coef[5] = jnp.where(axial_lane == 0, 0.0, axial)
+    coef[6] = jnp.zeros_like(inverse)
+    coef[7] = jnp.zeros_like(inverse)
+    coef_columns = jnp.transpose(coef[...].reshape(8 * 2 * SPANS, LANES))
+    cell_lanes = jnp.bitwise_and(lax.broadcasted_iota(jnp.int32, (LANES, WIDE), 1), 4 * SPANS - 1)
+    to_cells = jnp.where(
+        (cell_lanes == lax.broadcasted_iota(jnp.int32, (LANES, WIDE), 0)) & (cell_lanes < 2 * SPANS), 1.0, 0.0
+    )
+    inlet_inverse = exact_dot(coef_columns[0:8, :], to_cells)[0:1, :]
 
     spread_lanes = lax.broadcasted_iota(jnp.int32, (SPANS, WIDE), 1)
     spread_span = jnp.where(
@@ -220,35 +232,19 @@
         upper = jnp.where(first_wide == own_panel - 1.0, 1.0 - share_wide, 0.0)
         panel_weight[a] = lower + upper
 
-    for t in range(NT):
-        if shifts[t]:
-            panel_copy(t).wait_recv()
-            panel_rows[t : t + 1, :] = panel_recv[t, 0:1, :]
-    cells_wide = jnp.zeros(wide, F32)
-    for a in range(2):
-        shares = panel_weight[a] * panel_rows[0:NT, :]
-        shares = shares + pltpu.roll(shares, WIDE - SPANS, 1)
-        shares = shares + pltpu.roll(shares, WIDE - 2 * SPANS, 1)
-        if a:
-            shares = pltpu.roll(shares, a * SPANS, 1)
-        cells_wide = jnp.where(lane_panel == a, shares, cells_wide)
-    spread = jnp.where(same_field, exact_dot(instance_rows, cells_wide), 0.0)
-    gather_cells = jnp.where(
-        jnp.bitwise_and(lax.broadcasted_iota(jnp.int32, (WIDE, LANES), 0), 4 * SPANS - 1)
-        == lax.broadcasted_iota(jnp.int32, (WIDE, LANES), 1),
-        1.0,
-        0.0,
-    )
-    seam = exact_dot(spread, gather_cells)
-
     base[...] = jnp.zeros_like(base)
     for r in range(SPANS):
         for a in range(2):
             cell = a * SPANS + r
-            moved = pltpu.roll(seam, LANES - cell, 1) if cell else seam
-            moved = jnp.where(lane == 0, moved, 0.0)
-            plane = rhs[pl.ds(cell, ROWS, stride=2 * SPANS), :] + moved[0:ROWS]
+            plane = rhs[pl.ds(cell, ROWS, stride=2 * SPANS), :]
             base[r, a, 0:ROWS, :] = plane * coef[0, cell : cell + 1, :]
+
+    beside = (span > 0).astype(jnp.int32) + (span < nr - 1).astype(jnp.int32)
+    pl.semaphore_wait(barrier, len(partners) + beside)
+
+    for t in range(NT):
+        if shifts[t]:
+            panel_copy(t).start()
 
     def theta_copies(k, r):
         up = pltpu.make_async_remote_copy(
@@ -359,12 +355,125 @@
 
     lax.fori_loop(0, SPANS, first, 0)
 
+    for t in range(NT):
+        if shifts[t]:
+            panel_copy(t).wait_recv()
+            panel_rows[t : t + 1, :] = panel_recv[t, 0:1, :]
+    cells_wide = jnp.zeros(wide, F32)
+    for a in range(2):
+        shares = panel_weight[a] * panel_rows[0:NT, :]
+        shares = shares + pltpu.roll(shares, WIDE - SPANS, 1)
+        shares = shares + pltpu.roll(shares, WIDE - 2 * SPANS, 1)
+        if a:
+            shares = pltpu.roll(shares, a * SPANS, 1)
+        cells_wide = jnp.where(lane_panel == a, shares, cells_wide)
+    cells_wide = cells_wide * inlet_inverse
+    delta_send[0:NT, :] = cells_wide
+
+    def delta_copy(n, device):
+        return pltpu.make_async_remote_copy(
+            src_ref=delta_send,
+            dst_ref=delta_recv.at[n],
+            send_sem=delta_sems.at[0, n],
+            recv_sem=delta_sems.at[1, n],
+            device_id=device,
+            device_id_type=MESH,
+        )
+
+    from_left = delta_copy(0, at_sector(1))
+    from_right = delta_copy(1, at_sector(ns - 1))
+    from_lower = delta_copy(2, {"span": span + 1})
+    from_upper = delta_copy(3, {"span": span - 1})
+
+    @pl.when(span < nr - 1)
+    def _():
+        from_lower.start()
+
+    @pl.when(span > 0)
+    def _():
+        from_upper.start()
+
+    from_left.start()
+    from_right.start()
+    from_left.wait_recv()
+    from_right.wait_recv()
+
+    @pl.when(span > 0)
+    def _():
+        from_lower.wait_recv()
+
+    @pl.when(span < nr - 1)
+    def _():
+        from_upper.wait_recv()
+
+    slot = jnp.bitwise_and(lax.broadcasted_iota(jnp.int32, wide, 1), 4 * SPANS - 1)
+
+    def place(values, n, shift, low, high):
+        moved = pltpu.roll(delta_recv[n, 0:NT, :], shift % WIDE, 1)
+        return jnp.where((slot >= low) & (slot < high), moved, values)
+
+    around = place(cells_wide, 0, SPANS, 2 * SPANS, 3 * SPANS)
+    around = place(around, 1, 3 * SPANS, 3 * SPANS, 4 * SPANS)
+    beyond = jnp.zeros(wide, F32)
+    beyond = place(beyond, 2, 1 - SPANS, 0, 1)
+    beyond = place(beyond, 2, 2 - 2 * SPANS, 1, 2)
+    beyond = place(beyond, 3, 2, 2, 3)
+    beyond = place(beyond, 3, 3 - SPANS, 3, 4)
+    gather_slot = jnp.bitwise_and(lax.broadcasted_iota(jnp.int32, (WIDE, LANES), 0), 4 * SPANS - 1)
+    gather_lane = lax.broadcasted_iota(jnp.int32, (WIDE, LANES), 1)
+    columns = jnp.zeros((PAD, LANES), F32)
+    for values, offset in ((around, 0), (beyond, 4 * SPANS)):
+        spread = jnp.where(same_field, exact_dot(instance_rows, values), 0.0)
+        gather = jnp.where(gather_slot + offset == gather_lane, 1.0, 0.0)
+        columns = columns + exact_dot(spread, gather)
+    high, low = split(columns)
+    product = jnp.dot(weights[...], jnp.concatenate([high, low, high], axis=0), preferred_element_type=F32)
+
+    def moved_part(m, shift):
+        return pltpu.roll(product[m * PAD : (m + 1) * PAD, :], shift % LANES, 1)
+
+    def inlet_coefficient(n, axial_cell):
+        return pltpu.roll(coef_columns[axial_cell : axial_cell + 1, :], (LANES - 2 * SPANS * n) % LANES, 1)
+
+    first_half = lane < SPANS
+    along = jnp.where(first_half, moved_part(1, -SPANS), moved_part(1, -2 * SPANS))
+    along = along + jnp.where(first_half, moved_part(2, -2 * SPANS), moved_part(2, SPANS))
+    across = moved_part(3, -1)
+    across = jnp.where(lane == SPANS - 1, moved_part(3, -(3 * SPANS + 3)), across)
+    across = jnp.where(lane == 2 * SPANS - 1, moved_part(3, -(2 * SPANS + 4)), across)
+    below = moved_part(4, 1)
+    below = jnp.where(lane == 0, moved_part(4, -4 * SPANS), below)
+    below = jnp.where(lane == SPANS, moved_part(4, -(3 * SPANS + 1)), below)
+    coupled = inlet_coefficient(1, 0) * product[0:PAD, :]
+    coupled = coupled + inlet_coefficient(2, 0) * along
+    coupled = coupled + inlet_coefficient(3, 0) * (across + below)
+    delta_columns[...] = columns
+    delta_shift[0] = coupled
+    delta_shift[1] = inlet_coefficient(5, 1) * product[6 * PAD : 7 * PAD, :]
+
+    def second(i, carry):
+        r = row_at(i)
+        planes = []
+        for a in range(2):
+            shift = lax.rem(LANES - a * SPANS - r, LANES)
+            moved = pltpu.roll(delta_columns[...], shift, 1)
+            base[r, a] = base[r, a] + jnp.where(lane == 0, moved, 0.0)
+        for a, plane in enumerate(update(0, r)):
+            shift = lax.rem(LANES - a * SPANS - r, LANES)
+            plane = plane - jnp.where(lane == 0, pltpu.roll(delta_shift[0], shift, 1), 0.0)
+            shift = lax.rem(shift + 1, LANES)
+            planes.append(plane - jnp.where(lane == 1, pltpu.roll(delta_shift[1], shift, 1), 0.0))
+        emit(1, r, planes)
+        return carry
+
+    lax.fori_loop(0, SPANS, second, 0)
+
     def middle(i, carry):
-        k, r = i // SPANS, row_at(lax.rem(i, SPANS))
+        k, r = i // SPANS + 1, row_at(lax.rem(i, SPANS))
         emit(k + 1, r, update(k, r))
         return carry
 
-    lax.fori_loop(0, (SWEEPS - 1) * SPANS, middle, 0)
+    lax.fori_loop(0, (SWEEPS - 2) * SPANS, middle, 0)
 
     inlet[...] = jnp.zeros_like(inlet)
 
@@ -398,6 +507,17 @@
         if shifts[t]:
             panel_copy(t).wait_send()
             back_copy(t).wait_send()
+
+    from_left.wait_send()
+    from_right.wait_send()
+
+    @pl.when(span < nr - 1)
+    def _():
+        from_lower.wait_send()
+
+    @pl.when(span > 0)
+    def _():
+        from_upper.wait_send()
 
     def drain(i, carry):
         k, r = i // SPANS, lax.rem(i, SPANS)
@@ -456,7 +576,7 @@
         scratch_shapes=[pltpu.VMEM(x.shape, x.dtype) for x in inputs]
         + [
             pltpu.VMEM((NMAT * PAD, 3 * PAD), BF16),
-            pltpu.VMEM((6, 2 * SPANS, LANES), F32),
+            pltpu.VMEM((8, 2 * SPANS, LANES), F32),
             pltpu.VMEM(plane[1:], F32),
             pltpu.VMEM(plane, F32),
             pltpu.VMEM(plane, F32),
@@ -474,6 +594,11 @@
             pltpu.VMEM((PAD, LANES), F32),
             pltpu.VMEM((NT, 1, WIDE), F32),
             pltpu.VMEM((NT, 1, WIDE), F32),
+            pltpu.VMEM((48, 8), F32),
+            pltpu.VMEM((16, WIDE), F32),
+            pltpu.VMEM((4, 16, WIDE), F32),
+            pltpu.VMEM((PAD, LANES), F32),
+            pltpu.VMEM((2, PAD, LANES), F32),
             pltpu.SemaphoreType.DMA((len(inputs),)),
             pltpu.SemaphoreType.DMA((SWEEPS, SPANS, 2)),
             pltpu.SemaphoreType.DMA((SWEEPS, SPANS, 2)),
@@ -481,6 +606,7 @@
             pltpu.SemaphoreType.DMA((SWEEPS, 2)),
             pltpu.SemaphoreType.DMA((2, NT)),
             pltpu.SemaphoreType.DMA((2, NT)),
+            pltpu.SemaphoreType.DMA((2, 4)),
         ],
         compiler_params=pltpu.CompilerParams(
             collective_id=0, has_side_effects=True, vmem_limit_bytes=60 * 2**20

time: 49.6 us -> 48.2 us (0.972)
  the two profiles are of different devices: /device:TPU:7 before, /device:TPU:17 now
where the time goes in v2:
time: 48.2 us; the launch traced here: 48.1 us
  Pallas kernels  47.5 us (99%)
  between operations  0.64 us (1%)
    pallas_call x1, Pallas kernels, on_device(): pl.pallas_call(functools.partial(kernel, ns, nr), out_shape=(pltpu.VMEM((...  46.5 us
    pallas_call x1, Pallas kernels, on_device(): pl.pallas_call(store, out_shape=(jax.ShapeDtypeStruct((nt * nf, ct * span...  1 us

profile of v2, /device:TPU:17, one launch (start us, length us, event | category | flops | bytes accessed | tf_op | source)
XLA Modules:
  0.0 48.1 jit_solution(5654568032931024600)
XLA Ops:
  0.6 46.5 %shard_map.122 = (f32[16,80,128]{2,1,0:T(8,128)S(1)}, f32[224,11]{1,0:T(8,128)S(1)}) custom-call(f32[1232,128]{1,0:T(8,128)} %bitcast.18, f32[16,128]{1,0:T(8,128)} %bitcast.21, f32[3,16,128]{2,1,0:T(8,128)} %bitcast.20, f32[16,128]{1,0:T(8,128)} %bitcast.22, f32[3,7,7]{2,1,0:T(8,128)} %refs_4_.1, f32[3,7,7]{2,1,0:T(8,128)} %refs_5_.1, s32[16,128]{1,0:T(8,128)} %bitcast.23, ...), custom_call_target="tpu_custom_call" | custom-call | tf_op jit(solution)/shard_map/pallas_call | solution.py:568
  47.1 1.0 %shard_map.123 = (f32[77,16,128]{2,1,0:T(8,128)}, f32[224,11]{1,0:T(8,128)}) custom-call(f32[16,80,128]{2,1,0:T(8,128)S(1)} %get-tuple-element.6.planes, f32[224,11]{1,0:T(8,128)S(1)} %get-tuple-element.7.table), custom_call_target="tpu_custom_call" | custom-call | tf_op jit(solution)/shard_map/pallas_call | solution.py:615

commit v3 on v2

--- a/solution.py
+++ b/solution.py
@@ -68,13 +68,11 @@
         weights,
         coef,
         base,
-        t_buf,
+        own_buf,
         tu_buf,
         td_buf,
         ru_buf,
         rd_buf,
-        xu_buf,
-        xd_buf,
         su_buf,
         sd_buf,
         panel_send,
@@ -249,7 +247,7 @@
     def theta_copies(k, r):
         up = pltpu.make_async_remote_copy(
             src_ref=su_buf.at[k, r],
-            dst_ref=tu_buf.at[k, r, 1],
+            dst_ref=tu_buf.at[k, r],
             send_sem=theta_send.at[k, r, 0],
             recv_sem=theta_recv.at[k, r, 0],
             device_id=at_sector(ns - 1),
@@ -257,7 +255,7 @@
         )
         down = pltpu.make_async_remote_copy(
             src_ref=sd_buf.at[k, r],
-            dst_ref=td_buf.at[k, r, 0],
+            dst_ref=td_buf.at[k, r],
             send_sem=theta_send.at[k, r, 1],
             recv_sem=theta_recv.at[k, r, 1],
             device_id=at_sector(1),
@@ -285,75 +283,86 @@
             device_id_type=MESH,
         )
 
-    def row_at(i):
-        return lax.rem(i, 2) * (SPANS - 1 - 2 * (i // 2)) + i // 2
-
-    def emit(k, r, planes):
-        columns = []
-        for plane in planes:
-            high, low = split(plane)
-            columns.append(jnp.concatenate([high, low, high], axis=0))
-        data = jnp.concatenate(columns, axis=1)
-        product = jnp.dot(weights[...], data, preferred_element_type=F32)
-
-        def part(m, a):
-            return product[m * PAD : (m + 1) * PAD, a * LANES : (a + 1) * LANES]
-
-        su_buf[k, r] = part(1, 0)
-        sd_buf[k, r] = part(2, 1)
-        for copy in theta_copies(k, r):
-            copy.start()
-        for a in range(2):
-            ru_buf[k, r, a] = part(3, a)
-            rd_buf[k, r + 1, a] = part(4, a)
-
-        @pl.when((r == 0) & (span > 0))
+    def rows_at(i):
+        low = lax.rem(i + SPANS // 2 - 1, SPANS // 2)
+        return low, SPANS - 1 - low
+
+    def coefficient(n, r, a):
+        return coef[n, pl.ds(a * SPANS + r, 1), :]
+
+    def emit(k, rows, planes_of):
+        for r, planes in zip(rows, planes_of):
+            columns = []
+            for plane in planes:
+                high, low = split(plane)
+                columns.append(jnp.concatenate([high, low, high], axis=0))
+            data = jnp.concatenate(columns, axis=1)
+            products = [
+                jnp.dot(weights[start * PAD : stop * PAD, :], data, preferred_element_type=F32)
+                for start, stop in ((0, 4), (4, NMAT))
+            ]
+
+            def part(m, a):
+                m, product = (m, products[0]) if m < 4 else (m - 4, products[1])
+                return product[m * PAD : (m + 1) * PAD, a * LANES : (a + 1) * LANES]
+
+            su_buf[k, r] = part(1, 0)
+            sd_buf[k, r] = part(2, 1)
+            for a in range(2):
+                ru_buf[k, r, a] = part(3, a)
+                rd_buf[k, r + 1, a] = part(4, a)
+                total = base[r, a] - coefficient(1, r, a) * part(0, a)
+                total = total - coefficient(2, r, a) * (part(2, 0) if a else part(1, 1))
+                total = total - coefficient(4, r, a) * pltpu.roll(part(5, a), LANES - 1, 1)
+                own_buf[k, r, a] = total - coefficient(5, r, a) * pltpu.roll(part(6, a), 1, 1)
+
+        @pl.when((rows[0] == 0) & (span > 0))
         def _():
             to_lower_span(k).start()
 
-        @pl.when((r == SPANS - 1) & (span < nr - 1))
+        @pl.when((rows[0] == 0) & (span < nr - 1))
         def _():
             to_upper_span(k).start()
 
-        tu_buf[k, r, 0] = part(1, 1)
-        td_buf[k, r, 1] = part(2, 0)
-        for a in range(2):
-            t_buf[k, r, a] = part(0, a)
-            xu_buf[k, r, a] = part(5, a)
-            xd_buf[k, r, a] = part(6, a)
-
-    def update(k, r):
-        for copy in theta_copies(k, r):
-            copy.wait_recv()
-
-        @pl.when((r == SPANS - 1) & (span < nr - 1))
+        for r in rows:
+            for copy in theta_copies(k, r):
+                copy.start()
+
+    def update(k, rows):
+        for r in rows:
+            for copy in theta_copies(k, r):
+                copy.wait_recv()
+
+        @pl.when((rows[0] == 0) & (span < nr - 1))
         def _():
             to_lower_span(k).wait_recv()
 
-        @pl.when((r == 0) & (span > 0))
+        @pl.when((rows[0] == 0) & (span > 0))
         def _():
             to_upper_span(k).wait_recv()
 
-        planes = []
-        for a in range(2):
-
-            def coefficient(n):
-                return coef[n, pl.ds(a * SPANS + r, 1), :]
-
-            total = base[r, a] - coefficient(1) * t_buf[k, r, a]
-            total = total - coefficient(2) * (tu_buf[k, r, a] + td_buf[k, r, a])
-            total = total - coefficient(3) * (ru_buf[k, r + 1, a] + rd_buf[k, r, a])
-            total = total - coefficient(4) * pltpu.roll(xu_buf[k, r, a], LANES - 1, 1)
-            total = total - coefficient(5) * pltpu.roll(xd_buf[k, r, a], 1, 1)
-            planes.append(total)
-        return planes
+        planes_of = []
+        for r in rows:
+            planes = []
+            for a in range(2):
+                outside = td_buf if a == 0 else tu_buf
+                total = own_buf[k, r, a] - coefficient(2, r, a) * outside[k, r]
+                planes.append(total - coefficient(3, r, a) * (ru_buf[k, r + 1, a] + rd_buf[k, r, a]))
+            planes_of.append(planes)
+        return planes_of
 
     def first(i, carry):
-        r = row_at(i)
-        emit(0, r, [base[r, a] for a in range(2)])
+        rows = rows_at(i)
+        emit(0, rows, [[base[r, a] for a in range(2)] for r in rows])
         return carry
 
-    lax.fori_loop(0, SPANS, first, 0)
+    lax.fori_loop(0, SPANS // 2, first, 0)
+
+    cell_row = jnp.bitwise_and(lax.broadcasted_iota(jnp.int32, (4 * SPANS, 2 * WIDE), 0), 2 * SPANS - 1)
+    panel_lane = lax.broadcasted_iota(jnp.int32, (4 * SPANS, 2 * WIDE), 1)
+    panel_cell = jnp.bitwise_and(panel_lane, SPANS - 1) + jnp.where(panel_lane < WIDE, 0, SPANS)
+    to_panels = jnp.where(cell_row == panel_cell, 1.0, 0.0).astype(BF16)
+    rows_twice = jnp.concatenate([instance_columns, instance_columns], axis=1).astype(BF16)
 
     for t in range(NT):
         if shifts[t]:
@@ -398,14 +407,6 @@
     from_left.wait_recv()
     from_right.wait_recv()
 
-    @pl.when(span > 0)
-    def _():
-        from_lower.wait_recv()
-
-    @pl.when(span < nr - 1)
-    def _():
-        from_upper.wait_recv()
-
     slot = jnp.bitwise_and(lax.broadcasted_iota(jnp.int32, wide, 1), 4 * SPANS - 1)
 
     def place(values, n, shift, low, high):
@@ -414,84 +415,105 @@
 
     around = place(cells_wide, 0, SPANS, 2 * SPANS, 3 * SPANS)
     around = place(around, 1, 3 * SPANS, 3 * SPANS, 4 * SPANS)
-    beyond = jnp.zeros(wide, F32)
-    beyond = place(beyond, 2, 1 - SPANS, 0, 1)
-    beyond = place(beyond, 2, 2 - 2 * SPANS, 1, 2)
-    beyond = place(beyond, 3, 2, 2, 3)
-    beyond = place(beyond, 3, 3 - SPANS, 3, 4)
     gather_slot = jnp.bitwise_and(lax.broadcasted_iota(jnp.int32, (WIDE, LANES), 0), 4 * SPANS - 1)
     gather_lane = lax.broadcasted_iota(jnp.int32, (WIDE, LANES), 1)
-    columns = jnp.zeros((PAD, LANES), F32)
-    for values, offset in ((around, 0), (beyond, 4 * SPANS)):
-        spread = jnp.where(same_field, exact_dot(instance_rows, values), 0.0)
-        gather = jnp.where(gather_slot + offset == gather_lane, 1.0, 0.0)
-        columns = columns + exact_dot(spread, gather)
-    high, low = split(columns)
-    product = jnp.dot(weights[...], jnp.concatenate([high, low, high], axis=0), preferred_element_type=F32)
+    gather = jnp.where(gather_slot == gather_lane, 1.0, 0.0)
+
+    def to_columns(values):
+        return exact_dot(jnp.where(same_field, exact_dot(instance_rows, values), 0.0), gather)
+
+    def stacked(columns):
+        high, low = split(columns)
+        return jnp.concatenate([high, low, high], axis=0)
+
+    def inlet_coefficient(n, axial_cell):
+        return pltpu.roll(coef_columns[axial_cell : axial_cell + 1, :], (LANES - 2 * SPANS * n) % LANES, 1)
+
+    columns = to_columns(around)
+    product = jnp.dot(weights[...], stacked(columns), preferred_element_type=F32)
 
     def moved_part(m, shift):
         return pltpu.roll(product[m * PAD : (m + 1) * PAD, :], shift % LANES, 1)
-
-    def inlet_coefficient(n, axial_cell):
-        return pltpu.roll(coef_columns[axial_cell : axial_cell + 1, :], (LANES - 2 * SPANS * n) % LANES, 1)
 
     first_half = lane < SPANS
     along = jnp.where(first_half, moved_part(1, -SPANS), moved_part(1, -2 * SPANS))
     along = along + jnp.where(first_half, moved_part(2, -2 * SPANS), moved_part(2, SPANS))
-    across = moved_part(3, -1)
-    across = jnp.where(lane == SPANS - 1, moved_part(3, -(3 * SPANS + 3)), across)
-    across = jnp.where(lane == 2 * SPANS - 1, moved_part(3, -(2 * SPANS + 4)), across)
-    below = moved_part(4, 1)
-    below = jnp.where(lane == 0, moved_part(4, -4 * SPANS), below)
-    below = jnp.where(lane == SPANS, moved_part(4, -(3 * SPANS + 1)), below)
+    across = jnp.where(jnp.bitwise_and(lane, SPANS - 1) == SPANS - 1, 0.0, moved_part(3, -1))
+    below = jnp.where(jnp.bitwise_and(lane, SPANS - 1) == 0, 0.0, moved_part(4, 1))
     coupled = inlet_coefficient(1, 0) * product[0:PAD, :]
     coupled = coupled + inlet_coefficient(2, 0) * along
     coupled = coupled + inlet_coefficient(3, 0) * (across + below)
     delta_columns[...] = columns
-    delta_shift[0] = coupled
+    delta_shift[0] = columns - coupled
     delta_shift[1] = inlet_coefficient(5, 1) * product[6 * PAD : 7 * PAD, :]
 
+    def beyond_span():
+        @pl.when(span > 0)
+        def _():
+            from_lower.wait_recv()
+
+        @pl.when(span < nr - 1)
+        def _():
+            from_upper.wait_recv()
+
+        cells = jnp.zeros(wide, F32)
+        for a in range(2):
+            top, bottom = (a + 1) * SPANS - 1, a * SPANS
+            cells = place(cells, 2, bottom - top, bottom, bottom + 1)
+            cells = place(cells, 3, top - bottom, top, top + 1)
+        product = jnp.dot(weights[3 * PAD : 5 * PAD, :], stacked(to_columns(cells)), preferred_element_type=F32)
+        above = jnp.where(jnp.bitwise_and(lane, SPANS - 1) == SPANS - 1, product[0:PAD], 0.0)
+        below = jnp.where(jnp.bitwise_and(lane, SPANS - 1) == 0, product[PAD : 2 * PAD], 0.0)
+        delta_shift[0] = delta_shift[0] - inlet_coefficient(3, 0) * (above + below)
+
     def second(i, carry):
-        r = row_at(i)
-        planes = []
-        for a in range(2):
-            shift = lax.rem(LANES - a * SPANS - r, LANES)
-            moved = pltpu.roll(delta_columns[...], shift, 1)
-            base[r, a] = base[r, a] + jnp.where(lane == 0, moved, 0.0)
-        for a, plane in enumerate(update(0, r)):
-            shift = lax.rem(LANES - a * SPANS - r, LANES)
-            plane = plane - jnp.where(lane == 0, pltpu.roll(delta_shift[0], shift, 1), 0.0)
-            shift = lax.rem(shift + 1, LANES)
-            planes.append(plane - jnp.where(lane == 1, pltpu.roll(delta_shift[1], shift, 1), 0.0))
-        emit(1, r, planes)
+        rows = rows_at(i)
+        planes_of = []
+        for r, planes in zip(rows, update(0, rows)):
+            corrected = []
+            for a, plane in enumerate(planes):
+                shift = lax.rem(LANES - a * SPANS - r, LANES)
+                moved = pltpu.roll(delta_columns[...], shift, 1)
+                base[r, a] = base[r, a] + jnp.where(lane == 0, moved, 0.0)
+                plane = plane + jnp.where(lane == 0, pltpu.roll(delta_shift[0], shift, 1), 0.0)
+                shift = lax.rem(shift + 1, LANES)
+                corrected.append(plane - jnp.where(lane == 1, pltpu.roll(delta_shift[1], shift, 1), 0.0))
+            planes_of.append(corrected)
+        emit(1, rows, planes_of)
         return carry
 
-    lax.fori_loop(0, SPANS, second, 0)
+    second(0, 0)
+    beyond_span()
+    lax.fori_loop(1, SPANS // 2, second, 0)
 
     def middle(i, carry):
-        k, r = i // SPANS + 1, row_at(lax.rem(i, SPANS))
-        emit(k + 1, r, update(k, r))
+        k, rows = i // (SPANS // 2) + 1, rows_at(lax.rem(i, SPANS // 2))
+        emit(k + 1, rows, update(k, rows))
         return carry
 
-    lax.fori_loop(0, (SWEEPS - 2) * SPANS, middle, 0)
+    lax.fori_loop(0, (SWEEPS - 2) * (SPANS // 2), middle, 0)
 
     inlet[...] = jnp.zeros_like(inlet)
 
     def last(i, carry):
-        r = row_at(i)
-        planes = update(SWEEPS - 1, r)
-        for a in range(2):
-            out[a * SPANS + r] = planes[a]
-            inlet[...] = jnp.where(lane == a * SPANS + r, pltpu.roll(planes[a], a * SPANS + r, 1), inlet[...])
+        rows = SPANS // 2 - 1 - i, SPANS // 2 + i
+        for r, planes in zip(rows, update(SWEEPS - 1, rows)):
+            for a in range(2):
+                out[a * SPANS + r] = planes[a]
+                inlet[...] = jnp.where(
+                    lane == a * SPANS + r, pltpu.roll(planes[a], a * SPANS + r, 1), inlet[...]
+                )
         return carry
 
-    lax.fori_loop(0, SPANS, last, 0)
-
-    back = jnp.zeros(wide, F32)
-    for a in range(2):
-        spread = exact_dot(inlet[:, a * SPANS : (a + 1) * SPANS], spread_span)
-        spread = jnp.where(same_field, spread, 0.0)
-        back = back + panel_weight[a] * exact_dot(instance_columns, spread)
+    lax.fori_loop(0, SPANS // 2, last, 0)
+
+    high, low = split(inlet[...])
+    cells = jnp.concatenate([high[:, 0 : 2 * SPANS], low[:, 0 : 2 * SPANS]], axis=1)
+    spread = jnp.dot(cells, to_panels, preferred_element_type=F32)
+    spread = jnp.where(jnp.concatenate([same_field, same_field], axis=1), spread, 0.0)
+    high, low = split(spread)
+    gathered = jnp.dot(rows_twice, jnp.concatenate([high, low], axis=0), preferred_element_type=F32)
+    back = panel_weight[0] * gathered[:, 0:WIDE] + panel_weight[1] * gathered[:, WIDE:]
     panel_rows[0:NT, :] = back
     for t in range(NT):
         if shifts[t]:
@@ -579,12 +601,10 @@
             pltpu.VMEM((8, 2 * SPANS, LANES), F32),
             pltpu.VMEM(plane[1:], F32),
             pltpu.VMEM(plane, F32),
-            pltpu.VMEM(plane, F32),
-            pltpu.VMEM(plane, F32),
+            pltpu.VMEM(edge, F32),
+            pltpu.VMEM(edge, F32),
             pltpu.VMEM(ring, F32),
             pltpu.VMEM(ring, F32),
-            pltpu.VMEM(plane, F32),
-            pltpu.VMEM(plane, F32),
             pltpu.VMEM(edge, F32),
             pltpu.VMEM(edge, F32),
             pltpu.VMEM((NT, 1, WIDE), F32),

time: 48.2 us -> 47.3 us (0.981)
  the two profiles are of different devices: /device:TPU:17 before, /device:TPU:38 now
where the time goes in v3:
time: 47.3 us; the launch traced here: 47.2 us
  Pallas kernels  46.6 us (99%)
  between operations  0.64 us (1%)
    pallas_call x1, Pallas kernels, on_device(): pl.pallas_call(functools.partial(kernel, ns, nr), out_shape=(pltpu.VMEM((...  45.6 us
    pallas_call x1, Pallas kernels, on_device(): pl.pallas_call(store, out_shape=(jax.ShapeDtypeStruct((nt * nf, ct * span...  1 us

profile of v3, /device:TPU:38, one launch (start us, length us, event | category | flops | bytes accessed | tf_op | source)
XLA Modules:
  0.0 47.2 jit_solution(9552132680223829460)
XLA Ops:
  0.6 45.6 %shard_map.122 = (f32[16,80,128]{2,1,0:T(8,128)S(1)}, f32[224,11]{1,0:T(8,128)S(1)}) custom-call(f32[1232,128]{1,0:T(8,128)} %bitcast.18, f32[16,128]{1,0:T(8,128)} %bitcast.21, f32[3,16,128]{2,1,0:T(8,128)} %bitcast.20, f32[16,128]{1,0:T(8,128)} %bitcast.22, f32[3,7,7]{2,1,0:T(8,128)} %refs_4_.1, f32[3,7,7]{2,1,0:T(8,128)} %refs_5_.1, s32[16,128]{1,0:T(8,128)} %bitcast.23, ...), custom_call_target="tpu_custom_call" | custom-call | tf_op jit(solution)/shard_map/pallas_call | solution.py:590
  46.2 1.0 %shard_map.123 = (f32[77,16,128]{2,1,0:T(8,128)}, f32[224,11]{1,0:T(8,128)}) custom-call(f32[16,80,128]{2,1,0:T(8,128)S(1)} %get-tuple-element.6.planes, f32[224,11]{1,0:T(8,128)S(1)} %get-tuple-element.7.table), custom_call_target="tpu_custom_call" | custom-call | tf_op jit(solution)/shard_map/pallas_call | solution.py:635

commit v4 on v3

--- a/solution.py
+++ b/solution.py
@@ -10,6 +10,7 @@
 from jax.sharding import PartitionSpec as P
 
 SWEEPS = 4
+AHEAD = 2
 NT = 11
 NF = 7
 ROWS = NT * NF
@@ -95,6 +96,11 @@
         panel_sems,
         back_sems,
         delta_sems,
+        ahead_send,
+        ahead_recv,
+        ahead_sems,
+        edge_coef,
+        edge_coef_sems,
     ) = refs
     sector = lax.axis_index("sector")
     span = lax.axis_index("span")
@@ -283,6 +289,74 @@
             device_id_type=MESH,
         )
 
+    def beside_copy(source, target, sems, upward):
+        slot = 0 if upward else 1
+        return pltpu.make_async_remote_copy(
+            src_ref=source,
+            dst_ref=target.at[slot],
+            send_sem=sems.at[0, slot],
+            recv_sem=sems.at[1, slot],
+            device_id={"span": span + 1 if upward else span - 1},
+            device_id_type=MESH,
+        )
+
+    def coef_copy(upward):
+        return beside_copy(coef.at[3], edge_coef, edge_coef_sems, upward)
+
+    def ahead_copy(upward):
+        return beside_copy(ahead_send.at[int(upward)], ahead_recv, ahead_sems, upward)
+
+    @pl.when(span > 0)
+    def _():
+        coef_copy(False).start()
+
+    @pl.when(span < nr - 1)
+    def _():
+        coef_copy(True).start()
+
+    def send_ahead(k):
+        for upward, r in ((False, 0), (True, SPANS - 1)):
+            for a in range(2):
+                outside = td_buf if a == 0 else tu_buf
+                inside = rd_buf[k, r, a] if upward else ru_buf[k, r + 1, a]
+                total = own_buf[k, r, a] - coefficient(2, r, a) * outside[k, r]
+                ahead_send[int(upward), a] = total - coefficient(3, r, a) * inside
+
+        @pl.when(span > 0)
+        def _():
+            ahead_copy(False).start()
+
+        @pl.when(span < nr - 1)
+        def _():
+            ahead_copy(True).start()
+
+    def receive_ahead(k):
+        def complete(slot, r, terms, m):
+            columns = []
+            for a in range(2):
+                cell = a * SPANS + r
+                plane = ahead_recv[slot, a] - edge_coef[slot, cell : cell + 1, :] * terms[a]
+                high, low = split(plane)
+                columns.append(jnp.concatenate([high, low, high], axis=0))
+            data = jnp.concatenate(columns, axis=1)
+            return jnp.dot(weights[m * PAD : (m + 1) * PAD, :], data, preferred_element_type=F32)
+
+        @pl.when(span < nr - 1)
+        def _():
+            coef_copy(False).wait_recv()
+            ahead_copy(False).wait_recv()
+            product = complete(1, 0, [rd_buf[k - 1, SPANS, a] for a in range(2)], 3)
+            for a in range(2):
+                ru_buf[k, SPANS, a] = product[:, a * LANES : (a + 1) * LANES]
+
+        @pl.when(span > 0)
+        def _():
+            coef_copy(True).wait_recv()
+            ahead_copy(True).wait_recv()
+            product = complete(0, SPANS - 1, [ru_buf[k - 1, 0, a] for a in range(2)], 4)
+            for a in range(2):
+                rd_buf[k, 0, a] = product[:, a * LANES : (a + 1) * LANES]
+
     def rows_at(i):
         low = lax.rem(i + SPANS // 2 - 1, SPANS // 2)
         return low, SPANS - 1 - low
@@ -316,13 +390,15 @@
                 total = total - coefficient(4, r, a) * pltpu.roll(part(5, a), LANES - 1, 1)
                 own_buf[k, r, a] = total - coefficient(5, r, a) * pltpu.roll(part(6, a), 1, 1)
 
-        @pl.when((rows[0] == 0) & (span > 0))
-        def _():
-            to_lower_span(k).start()
-
-        @pl.when((rows[0] == 0) & (span < nr - 1))
-        def _():
-            to_upper_span(k).start()
+        if k != AHEAD:
+
+            @pl.when((rows[0] == 0) & (span > 0))
+            def _():
+                to_lower_span(k).start()
+
+            @pl.when((rows[0] == 0) & (span < nr - 1))
+            def _():
+                to_upper_span(k).start()
 
         for r in rows:
             for copy in theta_copies(k, r):
@@ -333,13 +409,27 @@
             for copy in theta_copies(k, r):
                 copy.wait_recv()
 
-        @pl.when((rows[0] == 0) & (span < nr - 1))
-        def _():
-            to_lower_span(k).wait_recv()
-
-        @pl.when((rows[0] == 0) & (span > 0))
-        def _():
-            to_upper_span(k).wait_recv()
+        if k == AHEAD - 1:
+
+            @pl.when(rows[0] == 0)
+            def _():
+                send_ahead(k)
+
+        if k == AHEAD:
+
+            @pl.when(rows[0] == 0)
+            def _():
+                receive_ahead(k)
+
+        else:
+
+            @pl.when((rows[0] == 0) & (span < nr - 1))
+            def _():
+                to_lower_span(k).wait_recv()
+
+            @pl.when((rows[0] == 0) & (span > 0))
+            def _():
+                to_upper_span(k).wait_recv()
 
         planes_of = []
         for r in rows:
@@ -486,12 +576,14 @@
     beyond_span()
     lax.fori_loop(1, SPANS // 2, second, 0)
 
-    def middle(i, carry):
-        k, rows = i // (SPANS // 2) + 1, rows_at(lax.rem(i, SPANS // 2))
-        emit(k + 1, rows, update(k, rows))
-        return carry
-
-    lax.fori_loop(0, (SWEEPS - 2) * (SPANS // 2), middle, 0)
+    for k in range(1, SWEEPS - 1):
+
+        def middle(i, carry, k=k):
+            rows = rows_at(i)
+            emit(k + 1, rows, update(k, rows))
+            return carry
+
+        lax.fori_loop(0, SPANS // 2, middle, 0)
 
     inlet[...] = jnp.zeros_like(inlet)
 
@@ -548,15 +640,21 @@
         return carry
 
     lax.fori_loop(0, SWEEPS * SPANS, drain, 0)
-    for k in range(SWEEPS):
-
-        @pl.when(span > 0)
-        def _():
-            to_lower_span(k).wait_send()
-
-        @pl.when(span < nr - 1)
-        def _():
-            to_upper_span(k).wait_send()
+    @pl.when(span > 0)
+    def _():
+        coef_copy(False).wait_send()
+        ahead_copy(False).wait_send()
+        for k in range(SWEEPS):
+            if k != AHEAD:
+                to_lower_span(k).wait_send()
+
+    @pl.when(span < nr - 1)
+    def _():
+        coef_copy(True).wait_send()
+        ahead_copy(True).wait_send()
+        for k in range(SWEEPS):
+            if k != AHEAD:
+                to_upper_span(k).wait_send()
 
 
 def store(planes, table, out, sens, sems):
@@ -627,6 +725,11 @@
             pltpu.SemaphoreType.DMA((2, NT)),
             pltpu.SemaphoreType.DMA((2, NT)),
             pltpu.SemaphoreType.DMA((2, 4)),
+            pltpu.VMEM((2, 2, PAD, LANES), F32),
+            pltpu.VMEM((2, 2, PAD, LANES), F32),
+            pltpu.SemaphoreType.DMA((2, 2)),
+            pltpu.VMEM((2, 2 * SPANS, LANES), F32),
+            pltpu.SemaphoreType.DMA((2, 2)),
         ],
         compiler_params=pltpu.CompilerParams(
             collective_id=0, has_side_effects=True, vmem_limit_bytes=60 * 2**20

time: 47.3 us -> 45.6 us (0.964)
  the two profiles are of different devices: /device:TPU:38 before, /device:TPU:32 now
where the time goes in v4:
time: 45.6 us; the launch traced here: 45.5 us
  Pallas kernels  44.9 us (98%)
  between operations  0.64 us (1%)
    pallas_call x1, Pallas kernels, on_device(): pl.pallas_call(functools.partial(kernel, ns, nr), out_shape=(pltpu.VMEM((...  43.9 us
    pallas_call x1, Pallas kernels, on_device(): pl.pallas_call(store, out_shape=(jax.ShapeDtypeStruct((nt * nf, ct * span...  1 us

profile of v4, /device:TPU:32, one launch (start us, length us, event | category | flops | bytes accessed | tf_op | source)
XLA Modules:
  0.0 45.5 jit_solution(500077670955458463)
XLA Ops:
  0.6 43.9 %shard_map.122 = (f32[16,80,128]{2,1,0:T(8,128)S(1)}, f32[224,11]{1,0:T(8,128)S(1)}) custom-call(f32[1232,128]{1,0:T(8,128)} %bitcast.18, f32[16,128]{1,0:T(8,128)} %bitcast.21, f32[3,16,128]{2,1,0:T(8,128)} %bitcast.20, f32[16,128]{1,0:T(8,128)} %bitcast.22, f32[3,7,7]{2,1,0:T(8,128)} %refs_4_.1, f32[3,7,7]{2,1,0:T(8,128)} %refs_5_.1, s32[16,128]{1,0:T(8,128)} %bitcast.23, ...), custom_call_target="tpu_custom_call" | custom-call | tf_op jit(solution)/shard_map/pallas_call | solution.py:688
  44.5 1.0 %shard_map.123 = (f32[77,16,128]{2,1,0:T(8,128)}, f32[224,11]{1,0:T(8,128)}) custom-call(f32[16,80,128]{2,1,0:T(8,128)S(1)} %get-tuple-element.6.planes, f32[224,11]{1,0:T(8,128)S(1)} %get-tuple-element.7.table), custom_call_target="tpu_custom_call" | custom-call | tf_op jit(solution)/shard_map/pallas_call | solution.py:738

commit v5 on v4

--- a/solution.py
+++ b/solution.py
@@ -358,7 +358,7 @@
                 rd_buf[k, 0, a] = product[:, a * LANES : (a + 1) * LANES]
 
     def rows_at(i):
-        low = lax.rem(i + SPANS // 2 - 1, SPANS // 2)
+        low = lax.rem(i + SPANS // 2 - 2, SPANS // 2)
         return low, SPANS - 1 - low
 
     def coefficient(n, r, a):
@@ -453,6 +453,13 @@
     panel_cell = jnp.bitwise_and(panel_lane, SPANS - 1) + jnp.where(panel_lane < WIDE, 0, SPANS)
     to_panels = jnp.where(cell_row == panel_cell, 1.0, 0.0).astype(BF16)
     rows_twice = jnp.concatenate([instance_columns, instance_columns], axis=1).astype(BF16)
+
+    half_column = jnp.bitwise_and(lax.broadcasted_iota(jnp.int32, (PAD, 32), 1), 15).astype(F32)
+    of_instance = over_fields(index_of((PAD, 32), 0))[0] == half_column
+    spread_rows = jnp.where(of_instance & (index_of((PAD, 32), 0) < ROWS), 1.0, 0.0).astype(BF16)
+    gather_slot = jnp.bitwise_and(lax.broadcasted_iota(jnp.int32, (2 * WIDE, LANES), 0), 4 * SPANS - 1)
+    gather_lane = lax.broadcasted_iota(jnp.int32, (2 * WIDE, LANES), 1)
+    gather = jnp.where(gather_slot == gather_lane, 1.0, 0.0).astype(BF16)
 
     for t in range(NT):
         if shifts[t]:
@@ -494,8 +501,6 @@
 
     from_left.start()
     from_right.start()
-    from_left.wait_recv()
-    from_right.wait_recv()
 
     slot = jnp.bitwise_and(lax.broadcasted_iota(jnp.int32, wide, 1), 4 * SPANS - 1)
 
@@ -503,14 +508,11 @@
         moved = pltpu.roll(delta_recv[n, 0:NT, :], shift % WIDE, 1)
         return jnp.where((slot >= low) & (slot < high), moved, values)
 
-    around = place(cells_wide, 0, SPANS, 2 * SPANS, 3 * SPANS)
-    around = place(around, 1, 3 * SPANS, 3 * SPANS, 4 * SPANS)
-    gather_slot = jnp.bitwise_and(lax.broadcasted_iota(jnp.int32, (WIDE, LANES), 0), 4 * SPANS - 1)
-    gather_lane = lax.broadcasted_iota(jnp.int32, (WIDE, LANES), 1)
-    gather = jnp.where(gather_slot == gather_lane, 1.0, 0.0)
-
     def to_columns(values):
-        return exact_dot(jnp.where(same_field, exact_dot(instance_rows, values), 0.0), gather)
+        high, low = split(jnp.concatenate([values, jnp.zeros((16 - NT, WIDE), F32)], axis=0))
+        spread = jnp.dot(spread_rows, jnp.concatenate([high, low], axis=0), preferred_element_type=F32)
+        high, low = split(jnp.where(same_field, spread, 0.0))
+        return jnp.dot(jnp.concatenate([high, low], axis=1), gather, preferred_element_type=F32)
 
     def stacked(columns):
         high, low = split(columns)
@@ -519,15 +521,21 @@
     def inlet_coefficient(n, axial_cell):
         return pltpu.roll(coef_columns[axial_cell : axial_cell + 1, :], (LANES - 2 * SPANS * n) % LANES, 1)
 
-    columns = to_columns(around)
+    columns = to_columns(cells_wide)
     product = jnp.dot(weights[...], stacked(columns), preferred_element_type=F32)
+    from_left.wait_recv()
+    from_right.wait_recv()
+    around = place(jnp.zeros(wide, F32), 0, SPANS, 2 * SPANS, 3 * SPANS)
+    around = place(around, 1, 3 * SPANS, 3 * SPANS, 4 * SPANS)
+    around = jnp.dot(weights[PAD : 3 * PAD, :], stacked(to_columns(around)), preferred_element_type=F32)
+    around = pltpu.roll(around, LANES - 2 * SPANS, 1)
 
     def moved_part(m, shift):
         return pltpu.roll(product[m * PAD : (m + 1) * PAD, :], shift % LANES, 1)
 
     first_half = lane < SPANS
-    along = jnp.where(first_half, moved_part(1, -SPANS), moved_part(1, -2 * SPANS))
-    along = along + jnp.where(first_half, moved_part(2, -2 * SPANS), moved_part(2, SPANS))
+    along = jnp.where(first_half, moved_part(1, -SPANS), around[0:PAD])
+    along = along + jnp.where(first_half, around[PAD : 2 * PAD], moved_part(2, SPANS))
     across = jnp.where(jnp.bitwise_and(lane, SPANS - 1) == SPANS - 1, 0.0, moved_part(3, -1))
     below = jnp.where(jnp.bitwise_and(lane, SPANS - 1) == 0, 0.0, moved_part(4, 1))
     coupled = inlet_coefficient(1, 0) * product[0:PAD, :]
@@ -573,8 +581,9 @@
         return carry
 
     second(0, 0)
+    second(1, 0)
     beyond_span()
-    lax.fori_loop(1, SPANS // 2, second, 0)
+    lax.fori_loop(2, SPANS // 2, second, 0)
 
     for k in range(1, SWEEPS - 1):
 

time: 45.6 us -> 45 us (0.987)
  Pallas kernels: 44.9 us -> 44.3 us
    pallas_call x1, Pallas kernels: 43.9 us -> 43.3 us  [on_device(): pl.pallas_call(functools.partial(kernel, ns, nr), out_shape=(pltpu.VMEM((...]
where the time goes in v5:
time: 45 us; the launch traced here: 44.9 us
  Pallas kernels  44.3 us (98%)
  between operations  0.64 us (1%)
    pallas_call x1, Pallas kernels, on_device(): pl.pallas_call(functools.partial(kernel, ns, nr), out_shape=(pltpu.VMEM((...  43.3 us
    pallas_call x1, Pallas kernels, on_device(): pl.pallas_call(store, out_shape=(jax.ShapeDtypeStruct((nt * nf, ct * span...  1 us

profile of v5, /device:TPU:32, one launch (start us, length us, event | category | flops | bytes accessed | tf_op | source)
XLA Modules:
  0.0 44.9 jit_solution(15157035776425360582)
XLA Ops:
  0.6 43.3 %shard_map.122 = (f32[16,80,128]{2,1,0:T(8,128)S(1)}, f32[224,11]{1,0:T(8,128)S(1)}) custom-call(f32[1232,128]{1,0:T(8,128)} %bitcast.18, f32[16,128]{1,0:T(8,128)} %bitcast.21, f32[3,16,128]{2,1,0:T(8,128)} %bitcast.20, f32[16,128]{1,0:T(8,128)} %bitcast.22, f32[3,7,7]{2,1,0:T(8,128)} %refs_4_.1, f32[3,7,7]{2,1,0:T(8,128)} %refs_5_.1, s32[16,128]{1,0:T(8,128)} %bitcast.23, ...), custom_call_target="tpu_custom_call" | custom-call | tf_op jit(solution)/shard_map/pallas_call | solution.py:697
  43.9 1.0 %shard_map.123 = (f32[77,16,128]{2,1,0:T(8,128)}, f32[224,11]{1,0:T(8,128)}) custom-call(f32[16,80,128]{2,1,0:T(8,128)S(1)} %get-tuple-element.6.planes, f32[224,11]{1,0:T(8,128)S(1)} %get-tuple-element.7.table), custom_call_target="tpu_custom_call" | custom-call | tf_op jit(solution)/shard_map/pallas_call | solution.py:747

commit v6 on v5

--- a/solution.py
+++ b/solution.py
@@ -112,7 +112,8 @@
         return {"sector": lax.rem(sector + step, ns)}
 
     def load(n):
-        return pltpu.make_async_copy(hbm[n], vmem[n], input_sems.at[n])
+        target = vmem[n] if n else rhs.at[0 : ROWS * 2 * SPANS]
+        return pltpu.make_async_copy(hbm[n], target, input_sems.at[n])
 
     for n in (7, 0, 1, 6, 8, 9, 4, 5, 10, 2, 3):
         load(n).start()
@@ -702,7 +703,8 @@
         ),
         in_specs=[pl.BlockSpec(memory_space=pltpu.HBM)] * len(inputs),
         out_specs=(pl.BlockSpec(memory_space=pltpu.VMEM),) * 2,
-        scratch_shapes=[pltpu.VMEM(x.shape, x.dtype) for x in inputs]
+        scratch_shapes=[pltpu.VMEM((PAD * ct * spans, nax), F32)]
+        + [pltpu.VMEM(x.shape, x.dtype) for x in inputs[1:]]
         + [
             pltpu.VMEM((NMAT * PAD, 3 * PAD), BF16),
             pltpu.VMEM((8, 2 * SPANS, LANES), F32),

time: 45 us -> 45 us (level)
  no operation moved by 1% of the time
where the time goes in v6:
time: 45 us; the launch traced here: 44.9 us
  Pallas kernels  44.3 us (98%)
  between operations  0.64 us (1%)
    pallas_call x1, Pallas kernels, on_device(): pl.pallas_call(functools.partial(kernel, ns, nr), out_shape=(pltpu.VMEM((...  43.3 us
    pallas_call x1, Pallas kernels, on_device(): pl.pallas_call(store, out_shape=(jax.ShapeDtypeStruct((nt * nf, ct * span...  1 us

profile of v6, /device:TPU:32, one launch (start us, length us, event | category | flops | bytes accessed | tf_op | source)
XLA Modules:
  0.0 44.9 jit_solution(8773498203368211111)
XLA Ops:
  0.6 43.3 %shard_map.122 = (f32[16,80,128]{2,1,0:T(8,128)S(1)}, f32[224,11]{1,0:T(8,128)S(1)}) custom-call(f32[1232,128]{1,0:T(8,128)} %bitcast.18, f32[16,128]{1,0:T(8,128)} %bitcast.21, f32[3,16,128]{2,1,0:T(8,128)} %bitcast.20, f32[16,128]{1,0:T(8,128)} %bitcast.22, f32[3,7,7]{2,1,0:T(8,128)} %refs_4_.1, f32[3,7,7]{2,1,0:T(8,128)} %refs_5_.1, s32[16,128]{1,0:T(8,128)} %bitcast.23, ...), custom_call_target="tpu_custom_call" | custom-call | tf_op jit(solution)/shard_map/pallas_call | solution.py:698
  43.9 1.0 %shard_map.123 = (f32[77,16,128]{2,1,0:T(8,128)}, f32[224,11]{1,0:T(8,128)}) custom-call(f32[16,80,128]{2,1,0:T(8,128)S(1)} %get-tuple-element.6.planes, f32[224,11]{1,0:T(8,128)S(1)} %get-tuple-element.7.table), custom_call_target="tpu_custom_call" | custom-call | tf_op jit(solution)/shard_map/pallas_call | solution.py:749

commit v7 on v6

--- a/solution.py
+++ b/solution.py
@@ -374,11 +374,11 @@
             data = jnp.concatenate(columns, axis=1)
             products = [
                 jnp.dot(weights[start * PAD : stop * PAD, :], data, preferred_element_type=F32)
-                for start, stop in ((0, 4), (4, NMAT))
+                for start, stop in ((0, 3), (3, 5), (5, NMAT))
             ]
 
             def part(m, a):
-                m, product = (m, products[0]) if m < 4 else (m - 4, products[1])
+                m, product = (m, products[0]) if m < 3 else (m - 3, products[1]) if m < 5 else (m - 5, products[2])
                 return product[m * PAD : (m + 1) * PAD, a * LANES : (a + 1) * LANES]
 
             su_buf[k, r] = part(1, 0)

time: 45 us -> 45.1 us (level)
  no operation moved by 1% of the time
where the time goes in v7:
time: 45.1 us; the launch traced here: 45 us
  Pallas kernels  44.3 us (98%)
  between operations  0.64 us (1%)
    pallas_call x1, Pallas kernels, on_device(): pl.pallas_call(functools.partial(kernel, ns, nr), out_shape=(pltpu.VMEM((...  43.3 us
    pallas_call x1, Pallas kernels, on_device(): pl.pallas_call(store, out_shape=(jax.ShapeDtypeStruct((nt * nf, ct * span...  1 us

profile of v7, /device:TPU:32, one launch (start us, length us, event | category | flops | bytes accessed | tf_op | source)
XLA Modules:
  0.0 45.0 jit_solution(11793123677431471396)
XLA Ops:
  0.6 43.3 %shard_map.122 = (f32[16,80,128]{2,1,0:T(8,128)S(1)}, f32[224,11]{1,0:T(8,128)S(1)}) custom-call(f32[1232,128]{1,0:T(8,128)} %bitcast.18, f32[16,128]{1,0:T(8,128)} %bitcast.21, f32[3,16,128]{2,1,0:T(8,128)} %bitcast.20, f32[16,128]{1,0:T(8,128)} %bitcast.22, f32[3,7,7]{2,1,0:T(8,128)} %refs_4_.1, f32[3,7,7]{2,1,0:T(8,128)} %refs_5_.1, s32[16,128]{1,0:T(8,128)} %bitcast.23, ...), custom_call_target="tpu_custom_call" | custom-call | tf_op jit(solution)/shard_map/pallas_call | solution.py:698
  44.0 1.0 %shard_map.123 = (f32[77,16,128]{2,1,0:T(8,128)}, f32[224,11]{1,0:T(8,128)}) custom-call(f32[16,80,128]{2,1,0:T(8,128)S(1)} %get-tuple-element.6.planes, f32[224,11]{1,0:T(8,128)S(1)} %get-tuple-element.7.table), custom_call_target="tpu_custom_call" | custom-call | tf_op jit(solution)/shard_map/pallas_call | solution.py:749
